TPU v7x, 32 devices: a whole 2x2x4 slice. The times are simulated.
32 devices in a mesh: dp: 16 (over z, y, x), heads: 2 (over core).
Axes of the slice: x: 2, y: 2, z: 4, core: 2. Of those that a mesh axis runs over, the one named last changes fastest.
Arguments:
- tokens: bfloat16 [12288, 768], P('dp'), may hold values from -6 to 6
- memory: bfloat16 [12288, 768], P('dp'), may hold values from -6 to 6
- cotangent: bfloat16 [12288, 768], P(('dp', 'heads')), may hold values from -6 to 6
- seq_modes: int32 [32], replicated, may hold values from 0 to 2, as said below
- dec_lengths: int32 [32], replicated, may hold values from 192 to 384, as said below
- enc_lengths: int32 [32], replicated, may hold values from 96 to 384
- slot_plan: int32 [32], replicated, may hold values from 0 to 31, as said below
- buckets: int32 [384], replicated, may hold values from 0 to 31, as said below
- mode_table: bfloat16 [3, 768], P(None, 'dp'), may hold values from -6 to 6
- gain_self: bfloat16 [768], P('dp'), may hold values from 0.5 to 1.5
- gain_cross: bfloat16 [768], P('dp'), may hold values from 0.5 to 1.5
- gain_ffn: bfloat16 [768], P('dp'), may hold values from 0.5 to 1.5
- bucket_table: bfloat16 [32, 12], P(None, 'heads'), may hold values from -6 to 6
- self_query: bfloat16 [768, 768], P('dp', 'heads'), may hold values from -0.109375 to 0.109375
- self_key: bfloat16 [768, 768], P('dp', 'heads'), may hold values from -0.109375 to 0.109375
- self_value: bfloat16 [768, 768], P('dp', 'heads'), may hold values from -0.21875 to 0.21875
- self_output: bfloat16 [768, 768], P('heads', 'dp'), may hold values from -1.75 to 1.75
- cross_query: bfloat16 [768, 768], P('dp', 'heads'), may hold values from -0.109375 to 0.109375
- cross_key: bfloat16 [768, 768], P('dp', 'heads'), may hold values from -0.109375 to 0.109375
- cross_value: bfloat16 [768, 768], P('dp', 'heads'), may hold values from -0.21875 to 0.21875
- cross_output: bfloat16 [768, 768], P('heads', 'dp'), may hold values from -1.75 to 1.75
- ffn_gate: bfloat16 [768, 2048], P('dp', 'heads'), may hold values from -0.21875 to 0.21875
- ffn_up: bfloat16 [768, 2048], P('dp', 'heads'), may hold values from -0.21875 to 0.21875
- ffn_down: bfloat16 [2048, 768], P('heads', 'dp'), may hold values from -0.125 to 0.125
Outputs:
- layer_output: bfloat16 [12288, 768], P(('dp', 'heads'))
- tokens_grad: float32 [12288, 768], P('dp')
- memory_grad: float32 [12288, 768], P('dp')
- mode_table_grad: float32 [3, 768], P(None, 'dp')
- gain_self_grad: float32 [768], P('dp')
- gain_cross_grad: float32 [768], P('dp')
- gain_ffn_grad: float32 [768], P('dp')
- bucket_table_grad: float32 [32, 12], P(None, 'heads')
- self_query_grad: float32 [768, 768], P('dp', 'heads')
- self_key_grad: float32 [768, 768], P('dp', 'heads')
- self_value_grad: float32 [768, 768], P('dp', 'heads')
- self_output_grad: float32 [768, 768], P('heads', 'dp')
- cross_query_grad: float32 [768, 768], P('dp', 'heads')
- cross_key_grad: float32 [768, 768], P('dp', 'heads')
- cross_value_grad: float32 [768, 768], P('dp', 'heads')
- cross_output_grad: float32 [768, 768], P('heads', 'dp')
- ffn_gate_grad: float32 [768, 2048], P('dp', 'heads')
- ffn_up_grad: float32 [768, 2048], P('dp', 'heads')
- ffn_down_grad: float32 [2048, 768], P('heads', 'dp')
Inputs may be any that keep to these rules, and one draw needn't show every extreme that they name: `seq_modes`: all 2 sequences assigned to slots of one index of dp have the same mode. A permutation of the slots; sequence s is processed by index slot_plan[s] // 2 of dp. `dec_lengths`: the lengths of the 2 sequences assigned to one index of dp sum to 576. `buckets`: never falls as the distance grows; distance 0 is bucket 0.
All inputs are finite; a program needn't handle non-finite values.
Results may differ from a plain program's by a relative error of at most 0.024.
Values may be sent and summed in bfloat16 or wider, within the bound.
No kernel may reach another device: no remote copies, remote signals or barrier semaphores. Data moves between devices by JAX's collectives and lax.ppermute only.
A program may use at most 192 MiB of HBM per device.

v0:
```python
import jax
import jax.numpy as jnp
from jax import lax
from jax.sharding import PartitionSpec as P

norm_epsilon = 1e-06
masked_score = -1000000000.0
block_limit = 512
highest = lax.Precision.HIGHEST


def shortened(shard):

    def short(part):
        return part.astype(jnp.bfloat16) if part.dtype == jnp.float32 else part

    return jax.tree.map(short, shard)


def rms_norm(hidden, gain_row):
    return (
        hidden
        * lax.rsqrt(jnp.mean(hidden * hidden, axis=-1, keepdims=True) + norm_epsilon)
        * gain_row
    )


def gelu_tanh(values):
    return (
        0.5
        * values
        * (1.0 + jnp.tanh(0.7978845608028654 * (values + 0.044715 * values * values * values)))
    )


def gated_unit(gate_in, up_in):
    return gelu_tanh(gate_in) * up_in


def matmul(left_side, right_side):
    return jnp.dot(left_side, right_side, preferred_element_type=jnp.float32)


def matmul_left_t(left_side, right_side):
    return lax.dot_general(
        left_side, right_side, (((0,), (0,)), ((), ())), preferred_element_type=jnp.float32
    )


def matmul_right_t(left_side, right_side):
    return lax.dot_general(
        left_side, right_side, (((1,), (1,)), ((), ())), preferred_element_type=jnp.float32
    )


def toeplitz(window, height, breadth):
    length = window.shape[1]
    repeated = jnp.tile(window, (1, height + 1))
    folded = repeated[:, : height * (length + 1)].reshape(window.shape[0], height, length + 1)
    return folded[:, :, :breadth]


def distance_bias(table_dist, height):
    breadth = table_dist.shape[1]
    padded = jnp.concatenate(
        [jnp.zeros((table_dist.shape[0], breadth - 1), jnp.float32), table_dist], axis=1
    )
    return toeplitz(padded, height, breadth)[:, :, ::-1]


def distance_grad(grad_bias):
    heads_here, height, breadth = grad_bias.shape
    length = height + breadth - 1
    flipped = jnp.pad(grad_bias[:, :, ::-1], ((0, 0), (0, 0), (0, length + 1 - breadth)))
    flattened = jnp.pad(
        flipped.reshape(heads_here, height * (length + 1)), ((0, 0), (0, breadth - 1))
    )
    window_grad = jnp.sum(flattened.reshape(heads_here, height + 1, length), axis=1)
    return window_grad[:, breadth - 1 :]


def block_mask(first_row, height, breadth, length, causal):
    row_ids = first_row + jnp.arange(height)[:, None]
    col_ids = jnp.arange(breadth)[None, :]
    allowed = col_ids < length
    if causal:
        allowed = allowed & (col_ids <= row_ids)
    return allowed


def block_scores(query_block, key_one, table_dist, first_row, length, causal):
    height = query_block.shape[0]
    seq_len = key_one.shape[0]
    scores = jnp.einsum("qhd,khd->hqk", query_block, key_one, preferred_element_type=jnp.float32)
    if causal:
        scores = scores + distance_bias(table_dist, height)
    allowed = block_mask(first_row, height, seq_len, length, causal)
    return jnp.where(allowed[None], scores, masked_score)


def attention_forward(
    queries, key_rows, value_rows, lengths, table_dist, causal, sequences, heads_here
):
    total_rows, row_width = queries.shape
    seq_len = total_rows // sequences
    head_size = row_width // heads_here
    height = min(block_limit, seq_len)
    blocks = seq_len // height
    query_blocks = queries.reshape(sequences, blocks, height, heads_here, head_size)
    key_seq = key_rows.reshape(sequences, seq_len, heads_here, head_size)
    value_seq = value_rows.reshape(sequences, seq_len, heads_here, head_size)

    def one_sequence(inputs_seq):
        query_seq, key_one, value_one, length = inputs_seq

        def one_block(block_inputs):
            block_id, query_block = block_inputs
            scores = block_scores(
                query_block, key_one, table_dist, block_id * height, length, causal
            )
            largest = jnp.max(scores, axis=-1, keepdims=True)
            exponent = jnp.exp(scores - largest)
            totals = jnp.sum(exponent, axis=-1, keepdims=True)
            weights_low = (exponent / totals).astype(jnp.bfloat16)
            blended = jnp.einsum(
                "hqk,khd->qhd", weights_low, value_one, preferred_element_type=jnp.float32
            )
            return (
                blended.astype(jnp.bfloat16).reshape(height, row_width),
                (largest + jnp.log(totals))[:, :, 0],
            )

        return lax.map(one_block, (jnp.arange(blocks), query_seq))

    blended, log_totals = lax.map(one_sequence, (query_blocks, key_seq, value_seq, lengths))
    return (blended.reshape(total_rows, row_width), log_totals)


def attention_backward(
    queries,
    key_rows,
    value_rows,
    grad_out,
    log_totals,
    lengths,
    table_dist,
    causal,
    sequences,
    heads_here,
):
    total_rows, row_width = queries.shape
    seq_len = total_rows // sequences
    head_size = row_width // heads_here
    height = min(block_limit, seq_len)
    blocks = seq_len // height
    query_blocks = queries.reshape(sequences, blocks, height, heads_here, head_size)
    grad_blocks = grad_out.reshape(sequences, blocks, height, heads_here, head_size)
    key_seq = key_rows.reshape(sequences, seq_len, heads_here, head_size)
    value_seq = value_rows.reshape(sequences, seq_len, heads_here, head_size)

    def one_sequence(inputs_seq):
        query_seq, key_one, value_one, grad_seq, log_seq, length = inputs_seq

        def one_block(running, block_inputs):
            block_id, query_block, grad_block, log_block = block_inputs
            first_row = block_id * height
            scores = block_scores(query_block, key_one, table_dist, first_row, length, causal)
            weights_full = jnp.exp(scores - log_block[:, :, None])
            grad_weights = jnp.einsum(
                "qhd,khd->hqk", grad_block, value_one, preferred_element_type=jnp.float32
            )
            row_dots = jnp.sum(weights_full * grad_weights, axis=-1, keepdims=True)
            grad_scores = (weights_full * (grad_weights - row_dots)).astype(jnp.bfloat16)
            grad_query = jnp.einsum(
                "hqk,khd->qhd", grad_scores, key_one, preferred_element_type=jnp.float32
            )
            grad_keys = jnp.einsum(
                "hqk,qhd->khd", grad_scores, query_block, preferred_element_type=jnp.float32
            )
            grad_values = jnp.einsum(
                "hqk,qhd->khd",
                weights_full.astype(jnp.bfloat16),
                grad_block,
                preferred_element_type=jnp.float32,
            )
            key_sum, value_sum, bias_sum = running
            if causal:
                bias_sum = bias_sum + distance_grad(grad_scores.astype(jnp.float32))
            return (
                (key_sum + grad_keys, value_sum + grad_values, bias_sum),
                grad_query.reshape(height, row_width),
            )

        initial = (
            jnp.zeros((seq_len, heads_here, head_size), jnp.float32),
            jnp.zeros((seq_len, heads_here, head_size), jnp.float32),
            jnp.zeros((heads_here, seq_len), jnp.float32),
        )
        finals, grad_queries = lax.scan(
            one_block, initial, (jnp.arange(blocks), query_seq, grad_seq, log_seq)
        )
        return (grad_queries, finals[0], finals[1], finals[2])

    grad_queries, grad_keys, grad_values, bias_sums = lax.map(
        one_sequence, (query_blocks, key_seq, value_seq, grad_blocks, log_totals, lengths)
    )
    return (
        grad_queries.reshape(total_rows, row_width),
        grad_keys.reshape(total_rows, row_width),
        grad_values.reshape(total_rows, row_width),
        jnp.sum(bias_sums, axis=0),
    )


def regroup(token_rows, memory_rows, source_of, groups, per_group):
    row_width = token_rows.shape[1]
    piece_rows = token_rows.shape[0] // (per_group * groups)
    first_shaped = token_rows.reshape(per_group, groups, piece_rows, row_width)
    second_shaped = memory_rows.reshape(per_group, groups, piece_rows, row_width)
    spread_tokens, spread_memory = (
        lax.all_to_all(first_shaped, "dp", split_axis=1, concat_axis=0, tiled=True),
        lax.all_to_all(second_shaped, "dp", split_axis=1, concat_axis=0, tiled=True),
    )
    seq_total = per_group * groups
    ordered_tokens = jnp.take(
        spread_tokens.reshape(seq_total, piece_rows, row_width), source_of, axis=0
    )
    ordered_memory = jnp.take(
        spread_memory.reshape(seq_total, piece_rows, row_width), source_of, axis=0
    )
    ordered_tokens = ordered_tokens.reshape(groups, per_group, 1, piece_rows, row_width)
    ordered_memory = ordered_memory.reshape(groups, per_group, 1, piece_rows, row_width)
    joined_tokens, joined_memory = (
        lax.all_to_all(ordered_tokens, "dp", split_axis=0, concat_axis=2, tiled=True),
        lax.all_to_all(ordered_memory, "dp", split_axis=0, concat_axis=2, tiled=True),
    )
    return (joined_tokens.reshape(token_rows.shape), joined_memory.reshape(memory_rows.shape))


def restore(token_rows, memory_rows, slot_plan, groups, per_group):
    row_width = token_rows.shape[1]
    piece_rows = token_rows.shape[0] // (per_group * groups)
    first_shaped = token_rows.reshape(per_group, groups, piece_rows, row_width)
    second_shaped = memory_rows.reshape(per_group, groups, piece_rows, row_width)
    spread_tokens, spread_memory = (
        lax.all_to_all(
            shortened(first_shaped), "dp", split_axis=1, concat_axis=0, tiled=True
        ).astype(first_shaped.dtype),
        lax.all_to_all(
            shortened(second_shaped), "dp", split_axis=1, concat_axis=0, tiled=True
        ).astype(second_shaped.dtype),
    )
    seq_total = per_group * groups
    ordered_tokens = jnp.take(
        spread_tokens.reshape(seq_total, piece_rows, row_width), slot_plan, axis=0
    )
    ordered_memory = jnp.take(
        spread_memory.reshape(seq_total, piece_rows, row_width), slot_plan, axis=0
    )
    ordered_tokens = ordered_tokens.reshape(groups, per_group, 1, piece_rows, row_width)
    ordered_memory = ordered_memory.reshape(groups, per_group, 1, piece_rows, row_width)
    joined_tokens, joined_memory = (
        lax.all_to_all(
            shortened(ordered_tokens), "dp", split_axis=0, concat_axis=2, tiled=True
        ).astype(ordered_tokens.dtype),
        lax.all_to_all(
            shortened(ordered_memory), "dp", split_axis=0, concat_axis=2, tiled=True
        ).astype(ordered_memory.dtype),
    )
    return (joined_tokens.reshape(token_rows.shape), joined_memory.reshape(memory_rows.shape))


def join_rows(values):
    return lax.all_gather(values, "heads", axis=0, tiled=True)


def join_grads(values):
    return lax.all_gather(values, "heads", axis=0, tiled=True)


def join_final(values):
    return jax.tree.map(
        lambda part, own: part.astype(own.dtype),
        lax.all_gather(shortened(values), "heads", axis=0, tiled=True),
        values,
    )


def branch_sum(inputs, weight):
    return lax.psum_scatter(matmul(inputs, weight), "heads", scatter_dimension=0, tiled=True)


def rows_sum(term_fn, row_total):
    return lax.psum_scatter(
        term_fn(jnp.int32(0), lax.axis_size("heads") * row_total).astype(jnp.bfloat16),
        "heads",
        scatter_dimension=0,
        tiled=True,
    ).astype(jnp.float32)


def body(
    tokens,
    memory,
    cotangent,
    seq_modes,
    dec_lengths,
    enc_lengths,
    slot_plan,
    buckets,
    mode_table,
    gain_self,
    gain_cross,
    gain_ffn,
    bucket_table,
    self_query,
    self_key,
    self_value,
    self_output,
    cross_query,
    cross_key,
    cross_value,
    cross_output,
    ffn_gate,
    ffn_up,
    ffn_down,
):
    groups = lax.axis_size("dp")
    group_id = lax.axis_index("dp")
    halves = lax.axis_size("heads")
    half_id = lax.axis_index("heads")
    seq_total = slot_plan.shape[0]
    per_group = seq_total // groups
    seq_len = buckets.shape[0]
    model_width = tokens.shape[1]
    all_rows = per_group * seq_len
    own_rows = all_rows // halves
    own_seqs = per_group // halves
    heads_here = bucket_table.shape[1]
    bucket_count = bucket_table.shape[0]
    seq_ids = jnp.arange(seq_total, dtype=jnp.int32)
    placed = (slot_plan[:, None] == seq_ids[None, :]).astype(jnp.int32)
    source_of = jnp.sum(placed * seq_ids[:, None], axis=0)
    local_cols = lax.dynamic_slice_in_dim(placed, group_id * per_group, per_group, 1)
    modes_here = jnp.sum(local_cols * seq_modes[:, None], axis=0)
    dec_here = jnp.sum(local_cols * dec_lengths[:, None], axis=0)
    enc_here = jnp.sum(local_cols * enc_lengths[:, None], axis=0)
    (
        mode_full,
        gain_one,
        gain_two,
        gain_three,
        query_self,
        key_self,
        value_self,
        output_self,
        query_cross,
        key_cross,
        value_cross,
        output_cross,
        gate_full,
        up_full,
        down_full,
    ) = (
        lax.all_gather(mode_table, "dp", axis=1, tiled=True),
        lax.all_gather(gain_self, "dp", axis=0, tiled=True),
        lax.all_gather(gain_cross, "dp", axis=0, tiled=True),
        lax.all_gather(gain_ffn, "dp", axis=0, tiled=True),
        lax.all_gather(self_query, "dp", axis=0, tiled=True),
        lax.all_gather(self_key, "dp", axis=0, tiled=True),
        lax.all_gather(self_value, "dp", axis=0, tiled=True),
        lax.all_gather(self_output, "dp", axis=1, tiled=True),
        lax.all_gather(cross_query, "dp", axis=0, tiled=True),
        lax.all_gather(cross_key, "dp", axis=0, tiled=True),
        lax.all_gather(cross_value, "dp", axis=0, tiled=True),
        lax.all_gather(cross_output, "dp", axis=1, tiled=True),
        lax.all_gather(ffn_gate, "dp", axis=0, tiled=True),
        lax.all_gather(ffn_up, "dp", axis=0, tiled=True),
        lax.all_gather(ffn_down, "dp", axis=1, tiled=True),
    )
    gain_one_f = gain_one.astype(jnp.float32)
    gain_two_f = gain_two.astype(jnp.float32)
    gain_three_f = gain_three.astype(jnp.float32)
    bucket_onehot = (jnp.arange(bucket_count)[:, None] == buckets[None, :]).astype(jnp.bfloat16)
    table_dist = matmul(bucket_table.T, bucket_onehot)
    token_groups, memory_groups = regroup(tokens, memory, source_of, groups, per_group)
    own_tokens = lax.dynamic_slice_in_dim(token_groups, half_id * own_rows, own_rows, 0).astype(
        jnp.float32
    )
    own_modes = lax.dynamic_slice_in_dim(modes_here, half_id * own_seqs, own_seqs, 0)
    mode_onehot = (own_modes[:, None] == jnp.arange(mode_full.shape[0])[None, :]).astype(
        jnp.float32
    )
    mode_rows = matmul(mode_onehot.astype(jnp.bfloat16), mode_full)
    start_state = own_tokens + jnp.repeat(mode_rows, seq_len, axis=0)
    normed_one = join_rows(rms_norm(start_state, gain_one_f).astype(jnp.bfloat16))
    query_one = matmul(normed_one, query_self).astype(jnp.bfloat16)
    key_one = matmul(normed_one, key_self).astype(jnp.bfloat16)
    value_one = matmul(normed_one, value_self).astype(jnp.bfloat16)
    attended_one, log_one = attention_forward(
        query_one, key_one, value_one, dec_here, table_dist, True, per_group, heads_here
    )
    after_self = start_state + branch_sum(attended_one, output_self)
    normed_two = join_rows(rms_norm(after_self, gain_two_f).astype(jnp.bfloat16))
    query_two = matmul(normed_two, query_cross).astype(jnp.bfloat16)
    key_two = matmul(memory_groups, key_cross).astype(jnp.bfloat16)
    value_two = matmul(memory_groups, value_cross).astype(jnp.bfloat16)
    attended_two, log_two = attention_forward(
        query_two, key_two, value_two, enc_here, table_dist, False, per_group, heads_here
    )
    after_cross = after_self + branch_sum(attended_two, output_cross)
    normed_three = join_rows(rms_norm(after_cross, gain_three_f).astype(jnp.bfloat16))
    gate_pre = matmul(normed_three, gate_full)
    up_pre = matmul(normed_three, up_full)
    hidden = gated_unit(gate_pre, up_pre).astype(jnp.bfloat16)
    layer_output = (after_cross + branch_sum(hidden, down_full)).astype(jnp.bfloat16)
    grad_final = cotangent.astype(jnp.float32)
    grad_ffn_branch = join_grads(cotangent)
    grad_down = matmul_left_t(hidden, grad_ffn_branch)
    grad_hidden = matmul_right_t(grad_ffn_branch, down_full).astype(jnp.bfloat16)
    _, pull_unit = jax.vjp(gated_unit, gate_pre, up_pre)
    grad_gate_pre, grad_up_pre = pull_unit(grad_hidden.astype(jnp.float32))
    grad_gate_low = grad_gate_pre.astype(jnp.bfloat16)
    grad_up_low = grad_up_pre.astype(jnp.bfloat16)
    grad_gate = matmul_left_t(normed_three, grad_gate_low)
    grad_up = matmul_left_t(normed_three, grad_up_low)

    def ffn_term(first_row, row_count):
        return matmul_right_t(grad_gate_low, gate_full) + matmul_right_t(grad_up_low, up_full)

    grad_normed_three = rows_sum(ffn_term, own_rows)
    _, pull_three = jax.vjp(rms_norm, after_cross, gain_three_f)
    state_part, grad_gain_three = pull_three(grad_normed_three)
    grad_after_cross = grad_final + state_part
    grad_cross_branch = join_grads(grad_after_cross.astype(jnp.bfloat16))
    grad_output_cross = matmul_left_t(attended_two, grad_cross_branch)
    grad_attended_two = matmul_right_t(grad_cross_branch, output_cross).astype(jnp.bfloat16)
    grad_query_two, grad_key_two, grad_value_two, _ = attention_backward(
        query_two,
        key_two,
        value_two,
        grad_attended_two,
        log_two,
        enc_here,
        table_dist,
        False,
        per_group,
        heads_here,
    )
    grad_query_two = grad_query_two.astype(jnp.bfloat16)
    grad_key_two = grad_key_two.astype(jnp.bfloat16)
    grad_value_two = grad_value_two.astype(jnp.bfloat16)
    grad_query_cross = matmul_left_t(normed_two, grad_query_two)
    grad_key_cross = matmul_left_t(memory_groups, grad_key_two)
    grad_value_cross = matmul_left_t(memory_groups, grad_value_two)

    def cross_term(first_row, row_count):
        normed_part = matmul_right_t(grad_query_two, query_cross)
        memory_part = matmul_right_t(grad_key_two, key_cross) + matmul_right_t(
            grad_value_two, value_cross
        )
        return jnp.concatenate([normed_part, memory_part], axis=1)

    cross_sums = rows_sum(cross_term, own_rows)
    grad_normed_two = cross_sums[:, :model_width]
    grad_memory_own = cross_sums[:, model_width:]
    _, pull_two = jax.vjp(rms_norm, after_self, gain_two_f)
    state_part, grad_gain_two = pull_two(grad_normed_two)
    grad_after_self = grad_after_cross + state_part
    grad_self_branch = join_grads(grad_after_self.astype(jnp.bfloat16))
    grad_output_self = matmul_left_t(attended_one, grad_self_branch)
    grad_attended_one = matmul_right_t(grad_self_branch, output_self).astype(jnp.bfloat16)
    grad_query_one, grad_key_one, grad_value_one, distance_sums = attention_backward(
        query_one,
        key_one,
        value_one,
        grad_attended_one,
        log_one,
        dec_here,
        table_dist,
        True,
        per_group,
        heads_here,
    )
    grad_query_one = grad_query_one.astype(jnp.bfloat16)
    grad_key_one = grad_key_one.astype(jnp.bfloat16)
    grad_value_one = grad_value_one.astype(jnp.bfloat16)
    grad_query_self = matmul_left_t(normed_one, grad_query_one)
    grad_key_self = matmul_left_t(normed_one, grad_key_one)
    grad_value_self = matmul_left_t(normed_one, grad_value_one)

    def self_term(first_row, row_count):
        return (
            matmul_right_t(grad_query_one, query_self)
            + matmul_right_t(grad_key_one, key_self)
            + matmul_right_t(grad_value_one, value_self)
        )

    grad_normed_one = rows_sum(self_term, own_rows)
    _, pull_one = jax.vjp(rms_norm, start_state, gain_one_f)
    state_part, grad_gain_one = pull_one(grad_normed_one)
    grad_start = grad_after_self + state_part
    seq_sums = jnp.sum(grad_start.reshape(own_seqs, seq_len, model_width), axis=1)
    mode_grad = lax.dot_general(
        mode_onehot,
        seq_sums,
        (((0,), (0,)), ((), ())),
        precision=highest,
        preferred_element_type=jnp.float32,
    )
    table_local = lax.dot_general(
        bucket_onehot.astype(jnp.float32),
        distance_sums,
        (((1,), (1,)), ((), ())),
        precision=highest,
        preferred_element_type=jnp.float32,
    )
    table_whole = lax.dynamic_update_slice_in_dim(
        jnp.zeros((bucket_count, heads_here * halves), jnp.float32),
        table_local,
        half_id * heads_here,
        1,
    )
    gains_total, mode_total, table_total = lax.psum(
        (jnp.stack([grad_gain_one, grad_gain_two, grad_gain_three]), mode_grad, table_whole),
        ("dp", "heads"),
    )
    shard_width = model_width // groups
    gains_mine = lax.dynamic_slice_in_dim(gains_total, group_id * shard_width, shard_width, 1)
    mode_mine = lax.dynamic_slice_in_dim(mode_total, group_id * shard_width, shard_width, 1)
    table_mine = lax.dynamic_slice_in_dim(table_total, half_id * heads_here, heads_here, 1)
    start_whole, memory_whole = join_final((grad_start, grad_memory_own))
    tokens_grad, memory_grad = restore(start_whole, memory_whole, slot_plan, groups, per_group)
    weight_shards = (
        lax.psum_scatter(grad_query_self, "dp", scatter_dimension=0, tiled=True),
        lax.psum_scatter(grad_key_self, "dp", scatter_dimension=0, tiled=True),
        lax.psum_scatter(grad_value_self, "dp", scatter_dimension=0, tiled=True),
        lax.psum_scatter(grad_output_self, "dp", scatter_dimension=1, tiled=True),
        lax.psum_scatter(grad_query_cross, "dp", scatter_dimension=0, tiled=True),
        lax.psum_scatter(grad_key_cross, "dp", scatter_dimension=0, tiled=True),
        lax.psum_scatter(grad_value_cross, "dp", scatter_dimension=0, tiled=True),
        lax.psum_scatter(grad_output_cross, "dp", scatter_dimension=1, tiled=True),
        lax.psum_scatter(grad_gate, "dp", scatter_dimension=0, tiled=True),
        lax.psum_scatter(grad_up, "dp", scatter_dimension=0, tiled=True),
        lax.psum_scatter(grad_down, "dp", scatter_dimension=1, tiled=True),
    )
    return (
        layer_output,
        tokens_grad,
        memory_grad,
        mode_mine,
        gains_mine[0],
        gains_mine[1],
        gains_mine[2],
        table_mine,
        weight_shards[0],
        weight_shards[1],
        weight_shards[2],
        weight_shards[3],
        weight_shards[4],
        weight_shards[5],
        weight_shards[6],
        weight_shards[7],
        weight_shards[8],
        weight_shards[9],
        weight_shards[10],
    )


def solution(mesh):
    in_specs = (
        P("dp", None),
        P("dp", None),
        P(("dp", "heads"), None),
        P(),
        P(),
        P(),
        P(),
        P(),
        P(None, "dp"),
        P("dp"),
        P("dp"),
        P("dp"),
        P(None, "heads"),
        P("dp", "heads"),
        P("dp", "heads"),
        P("dp", "heads"),
        P("heads", "dp"),
        P("dp", "heads"),
        P("dp", "heads"),
        P("dp", "heads"),
        P("heads", "dp"),
        P("dp", "heads"),
        P("dp", "heads"),
        P("heads", "dp"),
    )
    out_specs = (
        P(("dp", "heads"), None),
        P("dp", None),
        P("dp", None),
        P(None, "dp"),
        P("dp"),
        P("dp"),
        P("dp"),
        P(None, "heads"),
        P("dp", "heads"),
        P("dp", "heads"),
        P("dp", "heads"),
        P("heads", "dp"),
        P("dp", "heads"),
        P("dp", "heads"),
        P("dp", "heads"),
        P("heads", "dp"),
        P("dp", "heads"),
        P("dp", "heads"),
        P("heads", "dp"),
    )
    return jax.shard_map(body, mesh=mesh, in_specs=in_specs, out_specs=out_specs, check_vma=False)
```

profile of v0, /device:TPU:0, one launch (start us, length us, event | category | flops | bytes accessed | tf_op | source)
XLA Modules:
  0.0 2776.6 jit_solution(4909308143654992519)
XLA Ops:
  87.5 51.3 %all-reduce.8 = (bf16[768]{0:T(1024)(128)(2,1)S(1)}, bf16[768]{0:T(1024)(128)(2,1)}, bf16[768]{0:T(1024)(128)(2,1)}) all-reduce(bf16[768]{0:T(1024)(128)(2,1)S(1)} %dynamic-update-slice, bf16[768]{0:T(1024)(128)(2,1)S(1)} %dynamic-update-slice.1, bf16[768]{0:T(1024)(128)(2,1)S(1)} %dynamic-update-slice.2), channel_id=1, replica_groups=mesh['dp'=16,'heads'=2] {'dp'}, use_global_device_ids=true, to_apply=%add.4 | all-reduce | flops 2304 | bytes 9216
  181.1 38.8 %all_gather.73 = bf16[768,384]{1,0:T(8,128)(2,1)S(1)} all-gather(bf16[48,384]{1,0:T(8,128)(2,1)S(1)} %copy-done.68), channel_id=1, replica_groups=mesh['dp'=16,'heads'=2] {'dp'}, dimensions={0}, use_global_device_ids=true | all-gather | bytes 626688 | tf_op jit(solution)/shard_map/all_gather | solution.py:369
  219.9 41.5 %all_gather.74 = bf16[768,384]{1,0:T(8,128)(2,1)S(1)} all-gather(bf16[48,384]{1,0:T(8,128)(2,1)S(1)} %copy-done.69), channel_id=1, replica_groups=mesh['dp'=16,'heads'=2] {'dp'}, dimensions={0}, use_global_device_ids=true | all-gather | bytes 626688 | tf_op jit(solution)/shard_map/all_gather | solution.py:370
  261.4 39.0 %all_gather.72 = bf16[768,384]{1,0:T(8,128)(2,1)S(1)} all-gather(bf16[48,384]{1,0:T(8,128)(2,1)S(1)} %copy-done.70), channel_id=1, replica_groups=mesh['dp'=16,'heads'=2] {'dp'}, dimensions={0}, use_global_device_ids=true | all-gather | bytes 626688 | tf_op jit(solution)/shard_map/all_gather | solution.py:371
  300.5 43.0 %all_gather.75 = bf16[384,768]{0,1:T(8,128)(2,1)} all-gather(bf16[384,48]{0,1:T(8,128)(2,1)S(1)} %copy-done.71), channel_id=1, replica_groups=mesh['dp'=16,'heads'=2] {'dp'}, dimensions={1}, use_global_device_ids=true | all-gather | bytes 626688 | tf_op jit(solution)/shard_map/all_gather | solution.py:372
  352.5 110.0 %while.51 = (s32[]{:T(128)}, bf16[2,1,384,384]{3,2,0,1:T(8,128)(2,1)}, f32[2,1,6,384]{3,2,1,0:T(8,128)}, bf16[2,384,6,64]{1,3,2,0:T(8,128)(2,1)}, s32[2]{0:T(128...) while((s32[]{:T(128)}, ...), condition=%wide.region_7.9_spmd, body=%wide.region_4.8_spmd.sunk | while | flops 234010752 | bytes 106621888 | solution.py:135
  470.6 50.9 %all_gather.79 = bf16[768,384]{1,0:T(8,128)(2,1)} all-gather(bf16[48,384]{1,0:T(8,128)(2,1)S(1)} %copy-done.72), channel_id=1, replica_groups=mesh['dp'=16,'heads'=2] {'dp'}, dimensions={0}, use_global_device_ids=true | all-gather | bytes 626688 | tf_op jit(solution)/shard_map/all_gather | solution.py:373
  524.8 41.3 %all_gather.80 = bf16[768,384]{1,0:T(8,128)(2,1)S(1)} all-gather(bf16[48,384]{1,0:T(8,128)(2,1)S(1)} %copy-done.73), channel_id=1, replica_groups=mesh['dp'=16,'heads'=2] {'dp'}, dimensions={0}, use_global_device_ids=true | all-gather | bytes 626688 | tf_op jit(solution)/shard_map/all_gather | solution.py:374
  604.8 42.9 %all_gather.81 = bf16[384,768]{0,1:T(8,128)(2,1)} all-gather(bf16[384,48]{0,1:T(8,128)(2,1)S(1)} %copy-done.75), channel_id=1, replica_groups=mesh['dp'=16,'heads'=2] {'dp'}, dimensions={1}, use_global_device_ids=true | all-gather | bytes 626688 | tf_op jit(solution)/shard_map/all_gather | solution.py:376
  697.2 61.7 %all-gather.23.cloned.1.call-done = bf16[1024,768]{0,1:T(8,128)(2,1)} async-done(((bf16[1024,48]{0,1:T(8,128)(2,1)}), bf16[1024,768]{0,1:T(8,128)(2,1)}) %all-gather.23.cloned.1.call-update) | async-done | bytes 1572880 | tf_op jit(solution)/shard_map/all_gather | solution.py:379
  763.2 55.1 %all-gather.21.cloned.1.call-done = bf16[768,1024]{1,0:T(8,128)(2,1)} async-done(((bf16[48,1024]{1,0:T(8,128)(2,1)}), bf16[768,1024]{1,0:T(8,128)(2,1)}) %all-gather.21.cloned.1.call-update) | async-done | bytes 1572880 | tf_op jit(solution)/shard_map/all_gather | solution.py:378
  833.2 57.0 %all-gather.19.cloned.1.call-done = bf16[768,1024]{1,0:T(8,128)(2,1)} async-done(((bf16[48,1024]{1,0:T(8,128)(2,1)}), bf16[768,1024]{1,0:T(8,128)(2,1)}) %all-gather.19.cloned.1.call-update) | async-done | bytes 1572880 | tf_op jit(solution)/shard_map/all_gather | solution.py:377
  1012.1 263.2 %while.54 = (s32[]{:T(128)}, bf16[2,1,384,384]{3,2,0,1:T(8,128)(2,1)}, bf16[2,384,6,64]{1,3,2,0:T(8,128)(2,1)}, bf16[2,384,6,64]{1,3,2,0:T(8,128)(2,1)}, f32[2,6...) while((s32[]{:T(128)}, ...), condition=%wide.region_28.30_spmd, body=%wide.region_25.29_spmd.sunk | while | flops 576253824 | bytes 221244448 | solution.py:204
  1445.9 44.4 %all-reduce.7 = (f32[3,768]{1,0:T(4,128)S(1)}, f32[3,768]{1,0:T(4,128)S(1)}, f32[32,12]{0,1:T(8,128)S(1)}) all-reduce(f32[3,768]{1,0:T(4,128)S(1)} %broadcast_multiply_fusion, f32[3,768]{1,0:T(4,128)S(1)} %pad_maximum_fusion.1, f32[32,12]{0,1:T(8,128)S(1)} %dynamic_update_slice.74), channel_id=1, replica_groups=mesh['dp'=16,'heads'=2] {'dp','heads'}, use_global_device_ids=true, to_apply=%region_32.35 | all-reduce | flops 4992 | bytes 39936 | tf_op jit(solution)/shard_map/psum | solution.py:524
  1495.3 99.9 %reduce-scatter.44.cloned.1.call-done = f32[384,48]{0,1:T(8,128)} async-done(((f32[384,768]{0,1:T(8,128)}), f32[384,48]{0,1:T(8,128)}) %reduce-scatter.44.cloned.1.call-update) | async-done | bytes 73744 | tf_op jit(solution)/shard_map/reduce_scatter | solution.py:542
  1595.2 127.9 %reduce-scatter.42.cloned.1.call-done = f32[48,384]{1,0:T(8,128)} async-done(((f32[768,384]{1,0:T(8,128)}), f32[48,384]{1,0:T(8,128)}) %reduce-scatter.42.cloned.1.call-update) | async-done | bytes 73744 | tf_op jit(solution)/shard_map/reduce_scatter | solution.py:541
  1723.1 128.0 %reduce-scatter.40.cloned.1.call-done = f32[48,384]{1,0:T(8,128)} async-done(((f32[768,384]{1,0:T(8,128)}), f32[48,384]{1,0:T(8,128)}) %reduce-scatter.40.cloned.1.call-update) | async-done | bytes 73744 | tf_op jit(solution)/shard_map/reduce_scatter | solution.py:540
  1851.1 135.4 %reduce-scatter.48.cloned.1.call-done = f32[48,1024]{1,0:T(8,128)} async-done(((f32[768,1024]{1,0:T(8,128)}), f32[48,1024]{1,0:T(8,128)}) %reduce-scatter.48.cloned.1.call-update) | async-done | bytes 196624 | tf_op jit(solution)/shard_map/reduce_scatter | solution.py:544
  1986.5 135.8 %reduce-scatter.46.cloned.1.call-done = f32[48,1024]{1,0:T(8,128)} async-done(((f32[768,1024]{1,0:T(8,128)}), f32[48,1024]{1,0:T(8,128)}) %reduce-scatter.46.cloned.1.call-update) | async-done | bytes 196624 | tf_op jit(solution)/shard_map/reduce_scatter | solution.py:543
  2122.3 135.3 %reduce-scatter.50.cloned.1.call-done = f32[1024,48]{0,1:T(8,128)} async-done(((f32[1024,768]{0,1:T(8,128)}), f32[1024,48]{0,1:T(8,128)}) %reduce-scatter.50.cloned.1.call-update) | async-done | bytes 196624 | tf_op jit(solution)/shard_map/reduce_scatter | solution.py:545
  2257.6 128.3 %reduce-scatter.36.cloned.1.call-done = f32[384,48]{0,1:T(8,128)} async-done(((f32[384,768]{0,1:T(8,128)}), f32[384,48]{0,1:T(8,128)}) %reduce-scatter.36.cloned.1.call-update) | async-done | bytes 73744 | tf_op jit(solution)/shard_map/reduce_scatter | solution.py:538
  2386.0 127.9 %reduce-scatter.34.cloned.1.call-done = f32[48,384]{1,0:T(8,128)} async-done(((f32[768,384]{1,0:T(8,128)}), f32[48,384]{1,0:T(8,128)}) %reduce-scatter.34.cloned.1.call-update) | async-done | bytes 73744 | tf_op jit(solution)/shard_map/reduce_scatter | solution.py:537
  2513.8 127.8 %reduce-scatter.30.cloned.1.call-done = f32[48,384]{1,0:T(8,128)} async-done(((f32[768,384]{1,0:T(8,128)}), f32[48,384]{1,0:T(8,128)}) %reduce-scatter.30.cloned.1.call-update) | async-done | bytes 73744 | tf_op jit(solution)/shard_map/reduce_scatter | solution.py:535
  2641.7 127.9 %reduce-scatter.32.cloned.1.call-done = f32[48,384]{1,0:T(8,128)} async-done(((f32[768,384]{1,0:T(8,128)}), f32[48,384]{1,0:T(8,128)}) %reduce-scatter.32.cloned.1.call-update) | async-done | bytes 73744 | tf_op jit(solution)/shard_map/reduce_scatter | solution.py:536
  (639 shorter events, 925.9 us)
Async XLA Ops:
  79.3 99.5 %all-to-all-start.1 = ((bf16[16,2,1,24,768]{4,3,1,2,0:T(8,128)(2,1)}), bf16[16,2,1,24,768]{4,3,1,2,0:T(8,128)(2,1)S(1)}, u32[]{:S(2)}, u32[]{:S(2)}) async-start(bf16[16,2,1,24,768]{4,3,1,2,0:T(8,128)(2,1)} %bitcast.44), calls=%async_computation.1 | async-start | bytes 2359296 | tf_op jit(solution)/shard_map/all_to_all | solution.py:234
  85.5 257.9 %all-gather.13.cloned.1.call-start = ((), (), s32[]{:S(2)}) async-start(), calls=%async_computation.25 | async-start | bytes 1769472 | tf_op jit(solution)/shard_map/all_gather | solution.py:274
  180.9 340.7 %reduce-scatter.18.cloned.1.call-start = ((), (), s32[]{:S(2)}) async-start(), calls=%async_computation.26 | async-start | bytes 3538944 | tf_op jit(solution)/shard_map/reduce_scatter | solution.py:290
  466.0 181.7 %all-to-all-start.3 = ((bf16[16,2,1,24,768]{4,3,1,2,0:T(8,128)(2,1)}), bf16[16,2,1,24,768]{4,3,1,2,0:T(8,128)(2,1)}, u32[]{:S(2)}, u32[]{:S(2)}) async-start(bf16[16,2,1,24,768]{4,3,1,2,0:T(8,128)(2,1)} %bitcast.61), calls=%async_computation.4 | async-start | bytes 2359296 | tf_op jit(solution)/shard_map/all_to_all | solution.py:235
  470.5 185.3 %all-gather.15.cloned.1.call-start = ((), (), s32[]{:S(2)}) async-start(), calls=%async_computation.27 | async-start | bytes 1769472 | tf_op jit(solution)/shard_map/all_gather | solution.py:274
  524.7 160.7 %reduce-scatter.20.cloned.1.call-start = ((), (), s32[]{:S(2)}) async-start(), calls=%async_computation.28 | async-start | bytes 3538944 | tf_op jit(solution)/shard_map/reduce_scatter | solution.py:290
  680.0 78.8 %all-gather.23.cloned.1.call-start = ((), (), s32[]{:S(2)}) async-start(), calls=%async_computation.32 | async-start | bytes 1671168 | tf_op jit(solution)/shard_map/all_gather | solution.py:379
  680.6 137.7 %all-gather.21.cloned.1.call-start = ((), (), s32[]{:S(2)}) async-start(), calls=%async_computation.31 | async-start | bytes 1671168 | tf_op jit(solution)/shard_map/all_gather | solution.py:378
  681.4 147.0 %all-gather.17.cloned.1.call-start = ((), (), s32[]{:S(2)}) async-start(), calls=%async_computation.29 | async-start | bytes 1769472 | tf_op jit(solution)/shard_map/all_gather | solution.py:274
  689.0 201.2 %all-gather.19.cloned.1.call-start = ((), (), s32[]{:S(2)}) async-start(), calls=%async_computation.30 | async-start | bytes 1671168 | tf_op jit(solution)/shard_map/all_gather | solution.py:377
  689.7 223.4 %reduce-scatter.24.cloned.1.call-start = ((), (), s32[]{:S(2)}) async-start(), calls=%async_computation.35 | async-start | bytes 1769472 | tf_op jit(solution)/shard_map/reduce_scatter | solution.py:294
  995.3 296.9 %reduce-scatter.28.cloned.1.call-start = ((), (), s32[]{:S(2)}) async-start(), calls=%async_computation.39 | async-start | bytes 1769472 | tf_op jit(solution)/shard_map/reduce_scatter | solution.py:294
  1296.5 198.8 %reduce-scatter.38.cloned.1.call-start = ((), (), s32[]{:S(2)}) async-start(), calls=%async_computation.46 | async-start | bytes 1253376 | tf_op jit(solution)/shard_map/reduce_scatter | solution.py:539
  1299.9 295.3 %reduce-scatter.44.cloned.1.call-start = ((), (), s32[]{:S(2)}) async-start(), calls=%async_computation.49 | async-start | bytes 1253376 | tf_op jit(solution)/shard_map/reduce_scatter | solution.py:542
  1303.3 419.8 %reduce-scatter.42.cloned.1.call-start = ((), (), s32[]{:S(2)}) async-start(), calls=%async_computation.48 | async-start | bytes 1253376 | tf_op jit(solution)/shard_map/reduce_scatter | solution.py:541
  1305.3 545.8 %reduce-scatter.40.cloned.1.call-start = ((), (), s32[]{:S(2)}) async-start(), calls=%async_computation.47 | async-start | bytes 1253376 | tf_op jit(solution)/shard_map/reduce_scatter | solution.py:540
  1307.2 679.3 %reduce-scatter.48.cloned.1.call-start = ((), (), s32[]{:S(2)}) async-start(), calls=%async_computation.51 | async-start | bytes 3342336 | tf_op jit(solution)/shard_map/reduce_scatter | solution.py:544
  1313.2 809.1 %reduce-scatter.46.cloned.1.call-start = ((), (), s32[]{:S(2)}) async-start(), calls=%async_computation.50 | async-start | bytes 3342336 | tf_op jit(solution)/shard_map/reduce_scatter | solution.py:543
  1319.0 938.6 %reduce-scatter.50.cloned.1.call-start = ((), (), s32[]{:S(2)}) async-start(), calls=%async_computation.52 | async-start | bytes 3342336 | tf_op jit(solution)/shard_map/reduce_scatter | solution.py:545
  1334.3 1051.7 %reduce-scatter.36.cloned.1.call-start = ((), (), s32[]{:S(2)}) async-start(), calls=%async_computation.45 | async-start | bytes 1253376 | tf_op jit(solution)/shard_map/reduce_scatter | solution.py:538
  1371.2 1142.6 %reduce-scatter.34.cloned.1.call-start = ((), (), s32[]{:S(2)}) async-start(), calls=%async_computation.44 | async-start | bytes 1253376 | tf_op jit(solution)/shard_map/reduce_scatter | solution.py:537
  1408.8 1232.9 %reduce-scatter.30.cloned.1.call-start = ((), (), s32[]{:S(2)}) async-start(), calls=%async_computation.42 | async-start | bytes 1253376 | tf_op jit(solution)/shard_map/reduce_scatter | solution.py:535
  1434.2 59.6 %all-to-all-start.5 = ((bf16[16,2,1,24,768]{4,3,1,2,0:T(8,128)(2,1)}), bf16[16,2,1,24,768]{4,3,1,2,0:T(8,128)(2,1)S(1)}, u32[]{:S(2)}, u32[]{:S(2)}) async-start(bf16[16,2,1,24,768]{4,3,1,2,0:T(8,128)(2,1)} %bitcast.75), calls=%async_computation.11 | async-start | bytes 2359296 | tf_op jit(solution)/shard_map/all_to_all | solution.py:263
  1441.6 1328.0 %reduce-scatter.32.cloned.1.call-start = ((), (), s32[]{:S(2)}) async-start(), calls=%async_computation.43 | async-start | bytes 1253376 | tf_op jit(solution)/shard_map/reduce_scatter | solution.py:536
  (150 other events, 4324.9 us)
Sparse Core Ops, SparseCore 0:
  686.8 10.3 all-gather.24
  699.8 59.0 all-gather.22
  761.6 56.5 all-gather.20
  820.4 7.9 all-gather.16
  831.2 59.0 all-gather.18
  905.7 7.3 reduce-scatter.23
  918.3 10.4 all-gather.26
  966.4 11.0 reduce-scatter.25
  980.4 11.0 reduce-scatter.21
  995.4 10.3 all-gather.28
  1282.4 9.8 reduce-scatter.27
  1293.6 10.4 all-gather.32
  1305.5 10.3 all-gather.30
  1321.1 145.3 reduce-scatter.37
  1471.8 123.2 reduce-scatter.43
  1600.3 122.7 reduce-scatter.41
  1728.4 122.6 reduce-scatter.39
  1856.7 129.8 reduce-scatter.47
  1992.1 130.1 reduce-scatter.45
  2127.7 129.8 reduce-scatter.49
  2263.0 122.9 reduce-scatter.35
  2391.1 122.6 reduce-scatter.33
  2519.0 122.6 reduce-scatter.29
  2647.0 122.5 reduce-scatter.31
  (4 shorter events, 23.7 us)
where the time goes:
time: 2790 us; the launch traced here: 2780 us
  waiting for transfers between devices  1650 us (59%)
  blocking collectives  470 us (17%)
  local copies, waits for them, and re-layouts  379 us (14%)
  matrix products  130 us (5%)
  starting transfers between devices  56.2 us (2%)
  other arithmetic  54.5 us (2%)
    reduce_scatter x1, waiting for transfers between devices, body(): lax.psum_scatter(grad_gate, 'dp', scatter_dimension=0, tiled=True)  136 us
    reduce_scatter x1, waiting for transfers between devices, body(): lax.psum_scatter(grad_up, 'dp', scatter_dimension=0, tiled=True)  135 us
    reduce_scatter x1, waiting for transfers between devices, body(): lax.psum_scatter(grad_down, 'dp', scatter_dimension=1, tiled=True)  135 us
    reduce_scatter x1, waiting for transfers between devices, body(): lax.psum_scatter(grad_output_self, 'dp', scatter_dimension=1, tiled=True)  128 us
    reduce_scatter x1, waiting for transfers between devices, body(): lax.psum_scatter(grad_key_cross, 'dp', scatter_dimension=0, tiled=True)  128 us
    reduce_scatter x1, waiting for transfers between devices, body(): lax.psum_scatter(grad_value_cross, 'dp', scatter_dimension=0, tiled=True)  128 us
    reduce_scatter x1, waiting for transfers between devices, body(): lax.psum_scatter(grad_key_self, 'dp', scatter_dimension=0, tiled=True)  128 us
    reduce_scatter x1, waiting for transfers between devices, body(): lax.psum_scatter(grad_value_self, 'dp', scatter_dimension=0, tiled=True)  128 us
  transfers between devices with their start and end apart: 36, of which 27 were waited for; matrix products, arithmetic and copies ran while one was open for 3% of the time, Pallas kernels for 0%

commit v1 on v0

v1 whole, which is shorter than its diff:
```python
import functools

import jax
import jax.numpy as jnp
from jax import lax
from jax.experimental import pallas as pl
from jax.experimental.pallas import tpu as pltpu
from jax.sharding import PartitionSpec as P

norm_epsilon = 1e-06
masked_score = -1000000000.0
lanes = 128
window_width = 512
cross_height = 384
highest = lax.Precision.HIGHEST
bf16 = jnp.bfloat16
f32 = jnp.float32


def kernel_params(limit_mib=56):
    return pltpu.CompilerParams(vmem_limit_bytes=limit_mib * 1024 * 1024)


def cost(flops, moved, special=0):
    return pl.CostEstimate(flops=1000, bytes_accessed=1000, transcendentals=0)


def matmul(left_side, right_side):
    return jnp.dot(left_side, right_side, preferred_element_type=f32)


def matmul_left_t(left_side, right_side):
    return lax.dot_general(
        left_side, right_side, (((0,), (0,)), ((), ())), preferred_element_type=f32
    )


def matmul_right_t(left_side, right_side):
    return lax.dot_general(
        left_side, right_side, (((1,), (1,)), ((), ())), preferred_element_type=f32
    )


def rms_scale(hidden):
    return lax.rsqrt(jnp.mean(hidden * hidden, axis=-1, keepdims=True) + norm_epsilon)


def swap_halves(values):
    return lax.ppermute(values, "heads", [(0, 1), (1, 0)])


def flip_low(values, groups, bits):
    return lax.ppermute(values, "dp", [(i, i ^ bits) for i in range(groups)])


def shift_high(values, groups, step):
    high = groups // 4
    pairs = []
    for source in range(groups):
        z, low = source // 4, source % 4
        pairs.append((source, ((z - step) % high) * 4 + low))
    return lax.ppermute(values, "dp", pairs)


def stepwise(groups):
    return groups % 4 == 0 and 1 < groups // 4 <= 4


def place_kernel(order_ref, own_ref, x_ref, y_ref, left_ref, right_ref, out_ref):
    high = own_ref.shape[0]
    half = left_ref.shape[2]
    z, low = order_ref[0], order_ref[1]
    for step in range(high):
        base = lax.rem(z + step, high) * 4
        out_ref[base + low] = own_ref[step]
        out_ref[base + (low ^ 1)] = x_ref[step]
        out_ref[base + (low ^ 2)] = y_ref[step]
        out_ref[base + (low ^ 3), :, :half] = left_ref[step]
        out_ref[base + (low ^ 3), :, half:] = right_ref[step]


def pin(*values):
    return lax.optimization_barrier(values)


def gather_high(shard, groups):
    if not stepwise(groups):
        return [shard]
    return [shard] + [shift_high(shard, groups, k) for k in range(1, groups // 4)]


def gather_near(stack, groups):
    if not stepwise(groups):
        return ()
    return flip_low(stack, groups, 1), flip_low(stack, groups, 2)


def gather_far(near, groups):
    if not stepwise(groups):
        return ()
    half = near[0].shape[2] // 2
    return (
        flip_low(near[0][:, :, :half], groups, 2),
        flip_low(near[1][:, :, half:], groups, 1),
    )


def gather_place(stack, near, far, groups, group_id):
    if not stepwise(groups):
        return lax.all_gather(stack[0], "dp", axis=0, tiled=True)
    rows, width = stack.shape[1:]
    order = jnp.stack([group_id // 4, group_id % 4]).astype(jnp.int32)
    (placed,) = call(
        place_kernel, order, (stack, *near, *far), [((groups, rows, width), stack.dtype)]
    )
    return placed.reshape(groups * rows, width)


def scatter_far(grad, groups):
    if not stepwise(groups):
        return ()
    return flip_low(grad[0], groups, 1), flip_low(grad[1], groups, 2)


def near_sums(grad, far, groups):
    if not stepwise(groups):
        return ()
    left, right = far
    nothing = jnp.zeros_like(left)
    for_x = grad[2][1].astype(f32) + jnp.concatenate([nothing, right], 2).astype(f32)
    for_y = grad[2][2].astype(f32) + jnp.concatenate([left, nothing], 2).astype(f32)
    return for_x.astype(bf16), for_y.astype(bf16)


def scatter_near(sums, groups):
    if not stepwise(groups):
        return ()
    return flip_low(sums[0], groups, 1), flip_low(sums[1], groups, 2)


def high_sums(grad, near, groups, group_id):
    if not stepwise(groups):
        return grad
    high = groups // 4
    z = group_id // 4
    plane = grad[2][0].astype(f32) + near[0].astype(f32) + near[1].astype(f32)
    plane_low = plane.astype(bf16)
    return [lax.dynamic_index_in_dim(plane, z, 0, keepdims=False)] + [
        lax.dynamic_index_in_dim(plane_low, (z - k) % high, 0, keepdims=False)
        for k in range(1, high)
    ]


def scatter_high(sums, groups):
    if not stepwise(groups):
        return [lax.psum_scatter(sums[0], "dp", scatter_dimension=0, tiled=True).astype(f32)]
    return [sums[0]] + [shift_high(sums[k], groups, k) for k in range(1, groups // 4)]


def scatter_sum(parts):
    return sum(part.astype(f32) for part in parts)


def reorder_kernel(order_ref, in_ref, out_ref):
    def one(i, carry):
        out_ref[i] = in_ref[order_ref[i]]
        return carry

    lax.fori_loop(0, out_ref.shape[0], one, 0)


def reorder(blocks, order):
    vmem = pl.BlockSpec(memory_space=pltpu.VMEM)
    return pl.pallas_call(
        reorder_kernel,
        out_shape=jax.ShapeDtypeStruct(blocks.shape, blocks.dtype),
        in_specs=[pl.BlockSpec(memory_space=pltpu.SMEM), vmem],
        out_specs=vmem,
        compiler_params=kernel_params(),
        cost_estimate=cost(0, 4 * blocks.size),
    )(order, blocks)


def both_kernel(half_ref, own_ref, other_ref, out_ref):
    length = own_ref.shape[0]
    half = half_ref[0]
    out_ref[pl.ds(pl.multiple_of(half * length, 8), length), :] = own_ref[...]
    out_ref[pl.ds(pl.multiple_of((1 - half) * length, 8), length), :] = other_ref[...]


def both_sequences(own, other, half_id):
    vmem = pl.BlockSpec(memory_space=pltpu.VMEM)
    return pl.pallas_call(
        both_kernel,
        out_shape=jax.ShapeDtypeStruct((2 * own.shape[0], own.shape[1]), own.dtype),
        in_specs=[pl.BlockSpec(memory_space=pltpu.SMEM), vmem, vmem],
        out_specs=vmem,
        compiler_params=kernel_params(),
        cost_estimate=cost(0, 16 * own.size),
    )(half_id.reshape(1), own, other)


def column_half(values, which):
    part = values.shape[-1] // 2
    return lax.dynamic_slice_in_dim(values, which * part, part, values.ndim - 1)


def sequence_pieces(rows, groups, half_id):
    length, width = rows.shape
    keep = column_half(rows, half_id)
    other = swap_halves(column_half(rows, 1 - half_id))
    first = half_id == 0
    pair = jnp.stack([jnp.where(first, keep, other), jnp.where(first, other, keep)])
    return pair.reshape(2, groups, length // groups, width // 2).transpose(1, 0, 2, 3)


def exchange(pieces):
    return lax.all_to_all(pieces, "dp", split_axis=0, concat_axis=0, tiled=True)


def ordered_pieces(pieces, order, groups):
    _, _, piece, part = pieces.shape
    mixed = reorder(pieces.reshape(2 * groups, piece, part), order)
    return mixed.reshape(groups, 2, piece, part)


def collect_pieces(mixed):
    groups, _, piece, part = mixed.shape
    return exchange(mixed).transpose(1, 0, 2, 3).reshape(2, groups * piece, part)


def join_columns(mine, theirs, half_id):
    first = half_id == 0
    return jnp.where(
        first, jnp.concatenate([mine, theirs], -1), jnp.concatenate([theirs, mine], -1)
    )


def dot_rows(left_side, right_side):
    return lax.dot_general(
        left_side, right_side, (((1,), (1,)), ((), ())), preferred_element_type=f32
    )


def head_lanes(values, which):
    lane = lax.broadcasted_iota(jnp.int32, values.shape, 1)
    keep = (lane < lanes // 2) if which == 0 else (lane >= lanes // 2)
    return jnp.where(keep, values, jnp.zeros_like(values))


def bias_blocks(window_ref, head):
    row = window_ref[pl.ds(head, 1), :]
    spread = jnp.broadcast_to(row, (lanes, window_width))
    return pltpu.roll(spread, 0, 1, stride=1, stride_axis=0)


def both_heads(values):
    return jnp.concatenate([head_lanes(values, 0), head_lanes(values, 1)], axis=0)


def join_heads(values):
    rows = values.shape[0] // 2
    lane = lax.broadcasted_iota(jnp.int32, (rows, lanes), 1)
    return jnp.where(lane < lanes // 2, values[:rows], values[rows:])


def masked_block(raw, biases, seq_len, length, first):
    height, count = raw.shape[0] // 2, raw.shape[1]
    if biases is not None:
        rows = []
        for bias in biases:
            for at in range(first, first + height, lanes):
                row = [bias[:, seq_len - lanes - at : seq_len]]
                if at + lanes < count:
                    row.append(jnp.full((lanes, count - at - lanes), masked_score, f32))
                rows.append(jnp.concatenate(row, axis=1))
        raw = raw + jnp.concatenate(rows, axis=0)
    column = lax.broadcasted_iota(jnp.int32, raw.shape, 1)
    return jnp.where(column < length, raw, masked_score)


def softmax_block(scores):
    exponent = jnp.exp(scores - jnp.max(scores, axis=1, keepdims=True))
    return exponent * (1.0 / jnp.sum(exponent, axis=1, keepdims=True))


def attend(causal, places, length, window_ref, inputs, outputs):
    seq_len, width = outputs[0].shape
    pairs = width // lanes
    height = lanes if causal else cross_height

    for side in range(2):
        query_ref, key_ref, value_ref = inputs[3 * side : 3 * side + 3]
        out_ref = outputs[side]

        def one_pair(pair, carry):
            at = [pl.multiple_of(place + pair * lanes, lanes) for place in places]
            here = pl.ds(pl.multiple_of(pair * lanes, lanes), lanes)
            biases = None
            if causal:
                head = side * 2 * pairs + 2 * pair
                biases = [bias_blocks(window_ref, head + a) for a in range(2)]
            for first in range(0, seq_len, height):
                count = first + height if causal else seq_len
                query = both_heads(query_ref[first : first + height, pl.ds(at[0], lanes)])
                raw = dot_rows(query, key_ref[:count, pl.ds(at[1], lanes)])
                weights = softmax_block(masked_block(raw, biases, seq_len, length, first)).astype(bf16)
                blended = jnp.dot(
                    weights, value_ref[:count, pl.ds(at[2], lanes)], preferred_element_type=f32
                )
                out_ref[first : first + height, here] = join_heads(blended).astype(bf16)
            return carry

        lax.fori_loop(0, pairs, one_pair, 0, unroll=True)


def diagonal_sums(block):
    rows, columns = block.shape
    wide = jnp.concatenate([block, jnp.zeros((rows, window_width - columns), f32)], axis=1)
    total = wide[0:8]
    for first in range(8, rows, 8):
        total = total + pltpu.roll(wide[first : first + 8], window_width - first, 1)
    row = lax.broadcasted_iota(jnp.int32, total.shape, 0)
    for bit in (1, 2, 4):
        total = jnp.where((row & bit) != 0, pltpu.roll(total, window_width - bit, 1), total)
    return jnp.sum(total, axis=0, keepdims=True)


def attend_back(causal, places, length, window_ref, inputs, outputs, sums_ref, key_sum, value_sum):
    seq_len, width = inputs[3].shape
    pairs = width // lanes
    height = cross_height

    for side in range(2):
        query_ref, key_ref, value_ref, grad_ref = inputs[4 * side : 4 * side + 4]
        query_out, key_out = outputs[2 * side : 2 * side + 2]

        def one_pair(pair, carry):
            at = [pl.multiple_of(place + pair * lanes, lanes) for place in places]
            here = pl.ds(pl.multiple_of(pair * lanes, lanes), lanes)
            head = side * 2 * pairs + 2 * pair
            biases = None
            if causal:
                biases = [bias_blocks(window_ref, head + a) for a in range(2)]
            sums = [None, None]
            for first in reversed(range(0, seq_len, height)):
                count = first + height if causal else seq_len
                query = both_heads(query_ref[first : first + height, pl.ds(at[0], lanes)])
                grad = both_heads(grad_ref[first : first + height, here])
                key = key_ref[:count, pl.ds(at[1], lanes)]
                value = value_ref[:count, pl.ds(at[2], lanes)]
                raw = dot_rows(query, key)
                weights = softmax_block(masked_block(raw, biases, seq_len, length, first))
                grad_weights = dot_rows(grad, value)
                dots = jnp.sum(weights * grad_weights, axis=1, keepdims=True)
                grad_scores = (weights * (grad_weights - dots)).astype(bf16)
                grad_query = jnp.dot(grad_scores, key, preferred_element_type=f32)
                query_out[first : first + height, pl.ds(at[0], lanes)] = join_heads(grad_query).astype(bf16)
                key_part = matmul_left_t(grad_scores, query)
                value_part = matmul_left_t(weights.astype(bf16), grad)
                if causal:
                    for a in range(2):
                        for inner in range(0, height, lanes):
                            row = first + inner
                            part = grad_scores[a * height + inner :][:lanes, : row + lanes].astype(f32)
                            start = seq_len - lanes - row
                            if sums[a] is None:
                                gap = [jnp.zeros((lanes, start), f32)] if start else []
                                sums[a] = jnp.concatenate(gap + [part], axis=1)
                            elif start == 0:
                                sums[a] = sums[a] + part
                            else:
                                sums[a] = jnp.concatenate(
                                    [sums[a][:, :start], sums[a][:, start:] + part], axis=1
                                )
                if count == seq_len and first + height == seq_len:
                    key_sum[...] = key_part
                    value_sum[...] = value_part
                else:
                    key_sum[:count] = key_sum[:count] + key_part
                    value_sum[:count] = value_sum[:count] + value_part
            key_out[:, pl.ds(at[1], lanes)] = key_sum[...].astype(bf16)
            key_out[:, pl.ds(at[2], lanes)] = value_sum[...].astype(bf16)
            if causal:
                for a in range(2):
                    sums_ref[pl.ds(head + a, 1), :] = diagonal_sums(sums[a])
            return carry

        lax.fori_loop(0, pairs, one_pair, 0, unroll=True)


def call(body_fn, info, arrays, shapes, scratch=(), flops=0, moved=0):
    vmem = pl.BlockSpec(memory_space=pltpu.VMEM)
    return pl.pallas_call(
        body_fn,
        out_shape=[jax.ShapeDtypeStruct(shape, dtype) for shape, dtype in shapes],
        in_specs=[pl.BlockSpec(memory_space=pltpu.SMEM)] + [vmem] * len(arrays),
        out_specs=[vmem] * len(shapes),
        scratch_shapes=list(scratch),
        compiler_params=kernel_params(),
        cost_estimate=cost(flops, moved),
    )(info, *arrays)


def dot(left_side, right_side):
    return jnp.dot(left_side, right_side, preferred_element_type=f32)


def norm_rows(state, gain_row):
    return (state * rms_scale(state) * gain_row).astype(bf16)


def self_kernel(
    width,
    modes,
    info,
    tokens,
    pack_own,
    pack_other,
    window,
    start,
    normed,
    qkv_own,
    qkv_other,
    attended_own,
    attended_other,
    rows,
):
    length = start.shape[0]
    rows[...] = pack_own[:, 3 * width :].astype(f32).T[:8]
    mode_row = jnp.zeros_like(rows[0:1, :])
    for m in range(modes):
        mode_row = mode_row + jnp.where(info[1] == m, rows[3 + m : 4 + m, :], 0.0)
    at = pl.ds(pl.multiple_of(info[0] * length, 16), length)
    start[...] = tokens[at, :].astype(f32) + mode_row
    normed[...] = norm_rows(start[...], rows[0:1, :])
    for pack, qkv in ((pack_own, qkv_own), (pack_other, qkv_other)):
        for first in range(0, 3 * width, width):
            qkv[:, first : first + width] = dot(
                normed[...], pack[:, first : first + width]
            ).astype(bf16)
    attend(
        True,
        (0, width, 2 * width),
        info[2],
        window,
        (qkv_own,) * 3 + (qkv_other,) * 3,
        (attended_own, attended_other),
    )


def cross_kernel(
    width,
    info,
    start,
    rows,
    attended_own,
    attended_other,
    pack_own,
    pack_other,
    memory,
    after_self,
    normed,
    q_own,
    q_other,
    kv_own,
    kv_other,
    crossed_own,
    crossed_other,
):
    length = start.shape[0]
    after_self[...] = (
        start[...]
        + dot_rows(attended_own[...], pack_own[:, :width])
        + dot_rows(attended_other[...], pack_other[:, :width])
    )
    normed[...] = norm_rows(after_self[...], rows[1:2, :])
    at = pl.ds(pl.multiple_of(info[0] * length, 16), length)
    for pack, q, kv in ((pack_own, q_own, kv_own), (pack_other, q_other, kv_other)):
        q[...] = dot(normed[...], pack[:, width : 2 * width]).astype(bf16)
        kv[:, :width] = dot(memory[at, :], pack[:, 2 * width : 3 * width]).astype(bf16)
        kv[:, width:] = dot(memory[at, :], pack[:, 3 * width : 4 * width]).astype(bf16)
    attend(
        False,
        (0, 0, width),
        info[3],
        None,
        (q_own, kv_own, kv_own, q_other, kv_other, kv_other),
        (crossed_own, crossed_other),
    )


def ffn_kernel(
    width,
    info,
    after_self,
    rows,
    crossed_own,
    crossed_other,
    pack_own,
    pack_other,
    cot,
    after_cross,
    normed,
    hidden_own,
    hidden_other,
    grad_pre_own,
    grad_pre_other,
    output,
    total,
):
    hidden_width = hidden_own.shape[1]
    after_cross[...] = (
        after_self[...]
        + dot_rows(crossed_own[...], pack_own[:, :width])
        + dot_rows(crossed_other[...], pack_other[:, :width])
    )
    normed[...] = norm_rows(after_cross[...], rows[2:3, :])
    total[...] = after_cross[...]
    sides = (
        (pack_own, hidden_own, grad_pre_own),
        (pack_other, hidden_other, grad_pre_other),
    )
    for pack, hidden, grad_pre in sides:
        for first in range(0, hidden_width, 256):
            here = slice(first, first + 256)
            there = slice(hidden_width + first, hidden_width + first + 256)
            at = width + first
            down = pack[:, at + 2 * hidden_width : at + 2 * hidden_width + 256]
            gate_pre = dot(normed[...], pack[:, at : at + 256])
            up_pre = dot(normed[...], pack[:, at + hidden_width : at + hidden_width + 256])
            grad_hidden = dot(cot[...], down).astype(bf16).astype(f32)
            square = gate_pre * gate_pre * 0.044715
            bend = jnp.tanh(0.7978845608028654 * (gate_pre + square * gate_pre))
            half_more = 0.5 * (1.0 + bend)
            gelu = gate_pre * half_more
            slope = half_more + 0.5 * gate_pre * (1.0 - bend * bend) * 0.7978845608028654 * (
                1.0 + 3.0 * square
            )
            low = (gelu * up_pre).astype(bf16)
            hidden[:, here] = low
            grad_pre[:, here] = (grad_hidden * up_pre * slope).astype(bf16)
            grad_pre[:, there] = (grad_hidden * gelu).astype(bf16)
            total[...] = total[...] + dot_rows(low, down)
    output[...] = total[...].astype(bf16)


def norm_back_rows(state, gain_row, grad_normed):
    scale = rms_scale(state)
    scaled = state * scale
    weighted = grad_normed * gain_row
    inner = jnp.mean(weighted * scaled, axis=-1, keepdims=True)
    return scale * (weighted - scaled * inner), jnp.sum(grad_normed * scaled, axis=0, keepdims=True)


def cross_back_kernel(
    width,
    info,
    rows,
    cot,
    after_cross,
    grad_pre_own,
    grad_pre_other,
    pack_own,
    pack_other,
    q_own,
    q_other,
    kv_own,
    kv_other,
    grad_state,
    branch,
    grad_q_own,
    grad_q_other,
    grad_kv_own,
    grad_kv_other,
    gains,
    grad_own,
    grad_other,
    key_sum,
    value_sum,
):
    gate_up = slice(width, width + grad_pre_own.shape[1])
    grad_normed = dot_rows(grad_pre_own[...], pack_own[:, gate_up]) + dot_rows(
        grad_pre_other[...], pack_other[:, gate_up]
    )
    part, gain = norm_back_rows(after_cross[...], rows[2:3, :], grad_normed)
    gains[...] = jnp.zeros_like(gains)
    gains[2:3, :] = gain
    grad_state[...] = cot[...].astype(f32) + part
    branch[...] = grad_state[...].astype(bf16)
    grad_own[...] = dot(branch[...], pack_own[:, :width]).astype(bf16)
    grad_other[...] = dot(branch[...], pack_other[:, :width]).astype(bf16)
    attend_back(
        False,
        (0, 0, width),
        info[3],
        None,
        (q_own, kv_own, kv_own, grad_own, q_other, kv_other, kv_other, grad_other),
        (grad_q_own, grad_kv_own, grad_q_other, grad_kv_other),
        None,
        key_sum,
        value_sum,
    )


def between_kernel(
    width,
    info,
    rows,
    after_self,
    grad_in,
    grad_q_own,
    grad_q_other,
    grad_kv_own,
    grad_kv_other,
    pack_own,
    pack_other,
    grad_state,
    branch,
    grad_own,
    grad_other,
    grad_memory,
    gains,
):
    grad_normed = dot_rows(grad_q_own[...], pack_own[:, width : 2 * width]) + dot_rows(
        grad_q_other[...], pack_other[:, width : 2 * width]
    )
    part, gain = norm_back_rows(after_self[...], rows[1:2, :], grad_normed)
    gains[...] = jnp.zeros_like(gains)
    gains[1:2, :] = gain
    grad_state[...] = grad_in[...] + part
    branch[...] = grad_state[...].astype(bf16)
    grad_own[...] = dot(branch[...], pack_own[:, :width]).astype(bf16)
    grad_other[...] = dot(branch[...], pack_other[:, :width]).astype(bf16)
    grad_memory[...] = dot_rows(grad_kv_own[...], pack_own[:, 2 * width :]) + dot_rows(
        grad_kv_other[...], pack_other[:, 2 * width :]
    )


def self_back_kernel(
    width,
    info,
    window,
    qkv_own,
    qkv_other,
    grad_own,
    grad_other,
    grad_qkv_own,
    grad_qkv_other,
    sums,
    key_sum,
    value_sum,
):
    attend_back(
        True,
        (0, width, 2 * width),
        info[2],
        window,
        (qkv_own,) * 3 + (grad_own,) + (qkv_other,) * 3 + (grad_other,),
        (grad_qkv_own, grad_qkv_own, grad_qkv_other, grad_qkv_other),
        sums,
        key_sum,
        value_sum,
    )


def start_kernel(
    width,
    modes,
    info,
    rows,
    start,
    grad_in,
    grad_qkv_own,
    grad_qkv_other,
    one_own,
    one_other,
    sums,
    hot,
    gains_two,
    gains_three,
    grad_start,
    small,
):
    heads_here = width // 64
    grad_normed = dot_rows(grad_qkv_own[...], one_own[:, : 3 * width]) + dot_rows(
        grad_qkv_other[...], one_other[:, : 3 * width]
    )
    part, gain = norm_back_rows(start[...], rows[0:1, :], grad_normed)
    grad_start[...] = grad_in[...] + part
    small[...] = jnp.zeros_like(small)
    small[0:8, :] = gains_two[...] + gains_three[...]
    small[0:1, :] = gain
    total = jnp.sum(grad_start[...], axis=0, keepdims=True)
    for m in range(modes):
        small[3 + m : 4 + m, :] = jnp.where(info[1] == m, total, 0.0)
    table = lax.dot_general(
        sums[...], hot[...], (((1,), (1,)), ((), ())), precision=highest, preferred_element_type=f32
    )
    first, second = table[:heads_here], table[heads_here : 2 * heads_here]
    is_first = info[0] == 0
    small[8 : 8 + heads_here, : hot.shape[0]] = jnp.where(is_first, first, second)
    small[8 + heads_here : 8 + 2 * heads_here, : hot.shape[0]] = jnp.where(is_first, second, first)


def small_block(small, rows):
    depth = small.shape[1]
    turned = jnp.concatenate([small[:8], jnp.zeros((lanes - 8, depth), f32)], axis=0).T
    table = jnp.concatenate([small[8:24, :lanes], jnp.zeros((lanes - 16, lanes), f32)], axis=0).T
    lane = lax.broadcasted_iota(jnp.int32, (rows, lanes), 1)
    table = pltpu.roll(table[:rows], 8, 1)
    parts = [
        jnp.where(lane < 8, turned[at : at + rows], table) for at in range(0, depth, rows)
    ]
    return parts


def grad_kernel(counts, with_small, info, *refs):
    total = len(counts)
    inputs, outputs, whole = refs[: 4 * total], refs[-4:-1], refs[-1]
    high, rows = whole.shape[0] // 4, whole.shape[1]
    start = 0
    for i in range(total):
        left_own, left_other, right_own, right_other = inputs[4 * i : 4 * i + 4]
        for first in range(0, counts[i], 384):
            count = min(384, counts[i] - first)
            here = slice(first, first + count)
            part = matmul_left_t(left_own[...], right_own[:, here])
            part = (part + matmul_left_t(left_other[...], right_other[:, here])).astype(bf16)
            for block in range(4 * high):
                whole[block, :, start + first : start + first + count] = part[
                    block * rows : (block + 1) * rows
                ]
        start += counts[i]
    if with_small:
        small_own, small_other = refs[4 * total : 4 * total + 2]
        parts = small_block(small_own[...] + small_other[...], rows)
        for block in range(4 * high):
            whole[block, :, start:] = parts[block].astype(bf16)
    low = info[4]
    left_ref, right_ref, mid_ref = outputs
    half = left_ref.shape[2]
    for z in range(high):
        left_ref[z] = whole[z * 4 + (low ^ 3), :, :half]
        right_ref[z] = whole[z * 4 + (low ^ 3), :, half:]
        for k in range(3):
            mid_ref[k, z] = whole[z * 4 + (low ^ k)]


def weight_grads(entries, info, groups, small=()):
    counts = [entry[2].shape[1] for entry in entries]
    width = sum(counts) + (lanes if small else 0)
    depth = entries[0][0].shape[1]
    length = entries[0][0].shape[0]
    if not stepwise(groups):
        parts = [
            matmul_left_t(
                jnp.concatenate([a, b], axis=0), jnp.concatenate([c, d], axis=0)
            ).astype(bf16)
            for a, b, c, d in entries
        ]
        if small:
            both = small[0] + small[1]
            table = jnp.pad(both[8:24, : depth // groups].T, ((0, 0), (0, lanes - 24)))
            block = jnp.concatenate([both[:8].T, jnp.tile(table, (groups, 1))], axis=1)
            parts.append(block.astype(bf16))
        return (jnp.concatenate(parts, axis=1),)
    high, rows = groups // 4, depth // groups
    return call(
        functools.partial(grad_kernel, counts, bool(small)),
        info,
        [value for entry in entries for value in entry] + list(small),
        [((high, rows, width // 2), bf16)] * 2 + [((3, high, rows, width), bf16)],
        [pltpu.VMEM((groups, rows, width), bf16)],
        4 * length * depth * width,
        4 * depth * width,
    )


def body(
    tokens,
    memory,
    cotangent,
    seq_modes,
    dec_lengths,
    enc_lengths,
    slot_plan,
    buckets,
    mode_table,
    gain_self,
    gain_cross,
    gain_ffn,
    bucket_table,
    self_query,
    self_key,
    self_value,
    self_output,
    cross_query,
    cross_key,
    cross_value,
    cross_output,
    ffn_gate,
    ffn_up,
    ffn_down,
):
    groups = lax.axis_size("dp")
    group_id = lax.axis_index("dp")
    half_id = lax.axis_index("heads")
    seq_total = slot_plan.shape[0]
    seq_len = buckets.shape[0]
    model_width = tokens.shape[1]
    shard_width = model_width // groups
    heads_here = bucket_table.shape[1]
    bucket_count = bucket_table.shape[0]
    modes = mode_table.shape[0]
    width = self_query.shape[1]
    hidden_width = ffn_gate.shape[1]
    own_seq = group_id * 2 + half_id

    small = jnp.concatenate([jnp.stack([gain_self, gain_cross, gain_ffn]), mode_table]).T
    small = jnp.pad(small, ((0, 0), (0, lanes - small.shape[1])))
    pack_one = jnp.concatenate([self_query, self_key, self_value, small], axis=1)
    pack_two = jnp.concatenate(
        [self_output.T, cross_query, cross_key, cross_value], axis=1
    )
    pack_three = jnp.concatenate([cross_output.T, ffn_gate, ffn_up, ffn_down.T], axis=1)

    seq_ids = jnp.arange(seq_total, dtype=jnp.int32)
    placed = (slot_plan[:, None] == seq_ids[None, :]).astype(jnp.int32)
    source_of = jnp.sum(placed * seq_ids[:, None], axis=0)
    chosen = (seq_ids == own_seq).astype(jnp.int32)
    facts = jnp.sum(jnp.stack([seq_modes, dec_lengths, enc_lengths]) * chosen[None, :], axis=1)
    info = jnp.concatenate(
        [half_id.reshape(1), facts, (group_id % 4).reshape(1), (group_id // 4).reshape(1)]
    ).astype(jnp.int32)

    table_rows = jnp.concatenate([bucket_table, swap_halves(bucket_table)], axis=1).T
    reach = seq_len - lanes
    hole = window_width - seq_len
    window_bucket = jnp.concatenate(
        [
            jnp.flip(buckets[: reach + 1]),
            jnp.full((hole,), -1, jnp.int32),
            jnp.flip(buckets[reach + 1 :]),
        ]
    )
    window_hot = (jnp.arange(bucket_count)[:, None] == window_bucket[None, :]).astype(bf16)
    window = matmul(table_rows, window_hot)
    window = jnp.where(window_bucket[None, :] < 0, masked_score, window)
    window = jnp.pad(window, ((0, 16 - 2 * heads_here), (0, 0)))

    def stacked(parts):
        return jnp.stack(parts) if stepwise(groups) else parts

    high_one = gather_high(pack_one, groups)
    high_one, pack_two, pack_three = pin(high_one, pack_two, pack_three)
    three_own = lax.all_gather(pack_three, "dp", axis=0, tiled=True)
    cot_pieces = sequence_pieces(cotangent, groups, half_id)
    stack_one = stacked(high_one)
    near_one = gather_near(stack_one, groups)
    high_two = gather_high(pack_two, groups)
    near_one, high_two, cot_pieces = pin(near_one, high_two, cot_pieces)
    far_one = gather_far(near_one, groups)
    cot_pieces = exchange(cot_pieces)
    stack_two = stacked(high_two)
    near_two = gather_near(stack_two, groups)
    one_own = gather_place(stack_one, near_one, far_one, groups, group_id)
    one_other = swap_halves(one_own)

    tall = (seq_len, model_width)
    (
        start_state,
        normed_one,
        qkv_own,
        qkv_other,
        attended_own,
        attended_other,
        rows,
    ) = call(
        functools.partial(self_kernel, width, modes),
        info,
        (tokens, one_own, one_other, window),
        [(tall, f32), (tall, bf16)]
        + [((seq_len, 3 * width), bf16)] * 2
        + [((seq_len, width), bf16)] * 2
        + [((8, model_width), f32)],
        (),
        12 * seq_len * model_width * width,
        16 * seq_len * model_width,
    )
    near_two, attended_own, attended_other, cot_pieces = pin(
        near_two, attended_own, attended_other, cot_pieces
    )
    far_two = gather_far(near_two, groups)
    cot_pair = collect_pieces(ordered_pieces(cot_pieces, slot_plan, groups))
    two_own = gather_place(stack_two, near_two, far_two, groups, group_id)
    two_own, cot_pair = pin(two_own, cot_pair)
    two_other = swap_halves(two_own)
    cot_pair_other = swap_halves(cot_pair)
    (
        after_self,
        normed_two,
        q_own,
        q_other,
        kv_own,
        kv_other,
        crossed_own,
        crossed_other,
    ) = call(
        functools.partial(cross_kernel, width),
        info,
        (start_state, rows, attended_own, attended_other, two_own, two_other, memory),
        [(tall, f32), (tall, bf16)]
        + [((seq_len, width), bf16)] * 2
        + [((seq_len, 2 * width), bf16)] * 2
        + [((seq_len, width), bf16)] * 2,
        (),
        16 * seq_len * model_width * width,
        16 * seq_len * model_width,
    )
    crossed_own, crossed_other, three_own = pin(crossed_own, crossed_other, three_own)
    three_other = swap_halves(three_own)
    cot_whole = join_columns(cot_pair, cot_pair_other, half_id)
    cot_own = lax.dynamic_index_in_dim(cot_whole, half_id, 0, keepdims=False)
    cot_other = lax.dynamic_index_in_dim(cot_whole, 1 - half_id, 0, keepdims=False)
    (
        after_cross,
        normed_three,
        hidden_own,
        hidden_other,
        grad_pre_own,
        grad_pre_other,
        seq_output,
    ) = call(
        functools.partial(ffn_kernel, width),
        info,
        (
            after_self,
            rows,
            crossed_own,
            crossed_other,
            three_own,
            three_other,
            cot_own,
        ),
        [(tall, f32), (tall, bf16)]
        + [((seq_len, hidden_width), bf16)] * 2
        + [((seq_len, 2 * hidden_width), bf16)] * 2
        + [(tall, bf16)],
        (pltpu.VMEM(tall, f32),),
        18 * seq_len * model_width * hidden_width,
        24 * model_width * hidden_width,
    )

    other_memory = lax.dynamic_slice_in_dim(memory, (1 - half_id) * seq_len, seq_len, 0)
    own_memory = lax.dynamic_slice_in_dim(memory, half_id * seq_len, seq_len, 0)
    ffn_grad = weight_grads(
        (
            (normed_three, swap_halves(normed_three), grad_pre_own, swap_halves(grad_pre_other)),
            (cot_own, cot_other, hidden_own, swap_halves(hidden_other)),
        ),
        info,
        groups,
    )
    ffn_grad, grad_pre_own, grad_pre_other, seq_output = pin(
        ffn_grad, grad_pre_own, grad_pre_other, seq_output
    )
    ffn_far = scatter_far(ffn_grad, groups)
    out_pieces = exchange(sequence_pieces(seq_output, groups, half_id))
    sum_scratch = [pltpu.VMEM((seq_len, lanes), f32)] * 2
    (
        grad_after_cross,
        cross_branch,
        grad_q_own,
        grad_q_other,
        grad_kv_own,
        grad_kv_other,
        gains_three,
    ) = call(
        functools.partial(cross_back_kernel, width),
        info,
        (
            rows,
            cot_own,
            after_cross,
            grad_pre_own,
            grad_pre_other,
            three_own,
            three_other,
            q_own,
            q_other,
            kv_own,
            kv_other,
        ),
        [(tall, f32), (tall, bf16)]
        + [((seq_len, width), bf16)] * 2
        + [((seq_len, 2 * width), bf16)] * 2
        + [((8, model_width), f32)],
        [pltpu.VMEM((seq_len, width), bf16)] * 2 + sum_scratch,
        16 * seq_len * model_width * hidden_width,
        16 * model_width * hidden_width,
    )
    ffn_far, grad_after_cross, grad_q_own, grad_q_other, out_pieces = pin(
        ffn_far, grad_after_cross, grad_q_own, grad_q_other, out_pieces
    )
    ffn_sums = near_sums(ffn_grad, ffn_far, groups)
    out_mixed = ordered_pieces(out_pieces, source_of, groups)
    ffn_sums, out_mixed, grad_after_cross, grad_q_own, grad_q_other = pin(
        ffn_sums, out_mixed, grad_after_cross, grad_q_own, grad_q_other
    )
    ffn_near = scatter_near(ffn_sums, groups)
    out_pair = collect_pieces(out_mixed)
    (
        grad_after_self,
        self_branch,
        grad_att_own,
        grad_att_other,
        grad_memory,
        gains_two,
    ) = call(
        functools.partial(between_kernel, width),
        info,
        (
            rows,
            after_self,
            grad_after_cross,
            grad_q_own,
            grad_q_other,
            grad_kv_own,
            grad_kv_other,
            two_own,
            two_other,
        ),
        [(tall, f32), (tall, bf16)]
        + [((seq_len, width), bf16)] * 2
        + [(tall, f32), ((8, model_width), f32)],
    )
    cross_grad = weight_grads(
        (
            (normed_two, swap_halves(normed_two), grad_q_own, swap_halves(grad_q_other)),
            (own_memory, other_memory, grad_kv_own, swap_halves(grad_kv_other)),
            (cross_branch, swap_halves(cross_branch), crossed_own, swap_halves(crossed_other)),
            (self_branch, swap_halves(self_branch), attended_own, swap_halves(attended_other)),
        ),
        info,
        groups,
    )
    ffn_near, cross_grad, grad_att_own, grad_att_other, out_pair = pin(
        ffn_near, cross_grad, grad_att_own, grad_att_other, out_pair
    )
    ffn_sums = high_sums(ffn_grad, ffn_near, groups, group_id)
    ffn_sums, grad_att_own, grad_att_other = pin(ffn_sums, grad_att_own, grad_att_other)
    cross_far = scatter_far(cross_grad, groups)
    ffn_high = scatter_high(ffn_sums, groups)
    grad_qkv_own, grad_qkv_other, distance_sums = call(
        functools.partial(self_back_kernel, width),
        info,
        (window, qkv_own, qkv_other, grad_att_own, grad_att_other),
        [((seq_len, 3 * width), bf16)] * 2 + [(window.shape, f32)],
        sum_scratch,
    )
    cross_far, grad_qkv_own, grad_qkv_other, grad_memory = pin(
        cross_far, grad_qkv_own, grad_qkv_other, grad_memory
    )
    cross_sums = near_sums(cross_grad, cross_far, groups)
    cross_sums, grad_qkv_own, grad_qkv_other = pin(cross_sums, grad_qkv_own, grad_qkv_other)
    cross_near = scatter_near(cross_sums, groups)
    grad_start, small = call(
        functools.partial(start_kernel, width, modes),
        info,
        (
            rows,
            start_state,
            grad_after_self,
            grad_qkv_own,
            grad_qkv_other,
            one_own,
            one_other,
            distance_sums,
            jnp.pad(window_hot.astype(f32), ((0, lanes - bucket_count), (0, 0))),
            gains_two,
            gains_three,
        ),
        [(tall, f32), ((24, model_width), f32)],
    )
    small_other = swap_halves(small)
    qkv_grad = weight_grads(
        ((normed_one, swap_halves(normed_one), grad_qkv_own, swap_halves(grad_qkv_other)),),
        info,
        groups,
        (small, small_other),
    )
    ffn_high, qkv_grad, grad_start, grad_memory = pin(ffn_high, qkv_grad, grad_start, grad_memory)
    qkv_far = scatter_far(qkv_grad, groups)
    ffn_mine = scatter_sum(ffn_high)
    memory_grad = both_sequences(grad_memory, swap_halves(grad_memory), half_id)
    out_mine = lax.dynamic_index_in_dim(out_pair, half_id, 0, keepdims=False)
    out_sent = lax.dynamic_index_in_dim(out_pair, 1 - half_id, 0, keepdims=False)
    layer_output = join_columns(out_mine, swap_halves(out_sent), half_id)
    cross_near, qkv_far, memory_grad, layer_output, grad_start = pin(
        cross_near, qkv_far, memory_grad, layer_output, grad_start
    )
    qkv_sums = near_sums(qkv_grad, qkv_far, groups)
    cross_sums = high_sums(cross_grad, cross_near, groups, group_id)
    qkv_sums, cross_sums, grad_start = pin(qkv_sums, cross_sums, grad_start)
    qkv_near = scatter_near(qkv_sums, groups)
    cross_high = scatter_high(cross_sums, groups)
    tokens_grad = both_sequences(grad_start, swap_halves(grad_start), half_id)
    qkv_near, tokens_grad, ffn_mine = pin(qkv_near, tokens_grad, ffn_mine)
    self_mine = scatter_sum(
        scatter_high(high_sums(qkv_grad, qkv_near, groups, group_id), groups)
    )
    cross_mine = scatter_sum(cross_high)
    small_mine = self_mine[:, 3 * width :]
    mine = small_mine[:, :8].T
    if shard_width >= bucket_count:
        table_total = small_mine[:bucket_count, 8:24]
    else:
        table_total = lax.psum(small[8:24, :bucket_count] + small_other[8:24, :bucket_count], "dp").T
    table_mine = lax.dynamic_slice_in_dim(table_total, half_id * heads_here, heads_here, 1)
    return (
        layer_output,
        tokens_grad,
        memory_grad,
        mine[3 : 3 + modes],
        mine[0],
        mine[1],
        mine[2],
        table_mine,
        self_mine[:, :width],
        self_mine[:, width : 2 * width],
        self_mine[:, 2 * width : 3 * width],
        cross_mine[:, 4 * width :].T,
        cross_mine[:, :width],
        cross_mine[:, width : 2 * width],
        cross_mine[:, 2 * width : 3 * width],
        cross_mine[:, 3 * width : 4 * width].T,
        ffn_mine[:, :hidden_width],
        ffn_mine[:, hidden_width : 2 * hidden_width],
        ffn_mine[:, 2 * hidden_width :].T,
    )


def solution(mesh):
    rows_dp = P("dp", None)
    columns = P("dp", "heads")
    rows_heads = P("heads", "dp")
    in_specs = (
        (rows_dp, rows_dp, P(("dp", "heads"), None))
        + (P(),) * 5
        + (P(None, "dp"), P("dp"), P("dp"), P("dp"), P(None, "heads"))
        + (columns, columns, columns, rows_heads) * 2
        + (columns, columns, rows_heads)
    )
    out_specs = (
        (P(("dp", "heads"), None), rows_dp, rows_dp)
        + (P(None, "dp"), P("dp"), P("dp"), P("dp"), P(None, "heads"))
        + (columns, columns, columns, rows_heads) * 2
        + (columns, columns, rows_heads)
    )
    return jax.shard_map(body, mesh=mesh, in_specs=in_specs, out_specs=out_specs, check_vma=False)
```

time: 2790 us -> 387 us (0.14)
  waiting for transfers between devices: 1650 us -> 122 us
  blocking collectives: 470 us -> 0 us
  local copies, waits for them, and re-layouts: 379 us -> 21.6 us
  matrix products: 130 us -> 0.13 us
  Pallas kernels: 0 us -> 123 us
  other arithmetic: 54.5 us -> 22.5 us
    reduce_scatter x17 -> x0, waiting for transfers between devices: 1310 us -> none  [the longest x1 136 us: body(): lax.psum_scatter(grad_gate, 'dp', scatter_dimension=0, tiled=True)]
    all_gather x9 -> x0, blocking collectives: 374 us -> none  [the longest x1 50.9 us: body(): lax.all_gather(cross_query, 'dp', axis=0, tiled=True)]
    all_gather x11 -> x1, waiting for transfers between devices: 212 us -> 0.01 us  [body(): three_own = lax.all_gather(pack_three, 'dp', axis=0, tiled=True)]
    rev x6 -> x1, local copies, waits for them, and re-layouts: 137 us -> 0.1 us  [body(): jnp.flip(buckets[reach + 1:])]
    dot_general x64 -> x1, matrix products: 130 us -> 0.13 us  [matmul(): return jnp.dot(left_side, right_side, preferred_element_type=f32)]
    pallas_call x0 -> x16, Pallas kernels: none -> 123 us  [the longest x12 112 us: call(): pl.pallas_call(body_fn, out_shape=[jax.ShapeDtypeStruct(shape, dtype) for...]
    ppermute x0 -> x58, waiting for transfers between devices: none -> 116 us  [the longest x15 50.9 us: shift_high(): return lax.ppermute(values, 'dp', pairs)]
    all_to_all x8 -> x4, waiting for transfers between devices: 119 us -> 6.06 us  [exchange(): return lax.all_to_all(pieces, 'dp', split_axis=0, concat_axis=0, tiled=True)]
  transfers between devices with their start and end apart: 36 -> 63, of which waited for: 27 -> 29; matrix products, arithmetic and copies ran while one was open for 3% -> 6% of each run, Pallas kernels for 0% -> 26%
where the time goes in v1:
time: 387 us; the launch traced here: 379 us
  Pallas kernels  123 us (32%)
  waiting for transfers between devices  122 us (32%)
  starting transfers between devices  74.9 us (19%)
  other arithmetic  22.5 us (6%)
  local copies, waits for them, and re-layouts  21.6 us (6%)
  between operations  14.8 us (4%)
    pallas_call x12, Pallas kernels, call(): pl.pallas_call(body_fn, out_shape=[jax.ShapeDtypeStruct(shape, dtype) for...  112 us
    ppermute x15, waiting for transfers between devices, shift_high(): return lax.ppermute(values, 'dp', pairs)  50.9 us
    ppermute x20, waiting for transfers between devices, flip_low(): return lax.ppermute(values, 'dp', [(i, i ^ bits) for i in range(groups)])  42.4 us
    ppermute x20, starting transfers between devices, flip_low(): return lax.ppermute(values, 'dp', [(i, i ^ bits) for i in range(groups)])  25.2 us
    ppermute x15, starting transfers between devices, shift_high(): return lax.ppermute(values, 'dp', pairs)  22.9 us
    ppermute x23, waiting for transfers between devices, swap_halves(): return lax.ppermute(values, 'heads', [(0, 1), (1, 0)])  22.7 us
    all_to_all x4, starting transfers between devices, exchange(): return lax.all_to_all(pieces, 'dp', split_axis=0, concat_axis=0, tiled=True)  22.7 us
    unnamed x82, local copies, waits for them, and re-layouts  12.8 us
  transfers between devices with their start and end apart: 63, of which 29 were waited for; matrix products, arithmetic and copies ran while one was open for 6% of the time, Pallas kernels for 26%

profile of v1, /device:TPU:0, one launch (start us, length us, event | category | flops | bytes accessed | tf_op | source)
XLA Modules:
  0.0 379.2 jit_solution(7419034270224160313)
XLA Ops:
  8.9 5.1 %collective-permute-start = (bf16[48,1280]{1,0:T(8,128)(2,1)S(1)}, bf16[48,1280]{1,0:T(8,128)(2,1)S(1)}, u32[]{:S(2)}, u32[]{:S(2)}) collective-permute-start(bf16[48,1280]{1,0:T(8,128)(2,1)S(1)} %fusion.12), channel_id=1, source_target_pairs={{0,24},{2,26},{4,28},{6,30},{8,0},{10,2},{12,4},{14,6},{16,8},{18,... | collective-permute-start | bytes 368648 | tf_op jit(solution)/shard_map/ppermute | solution.py:62
  17.8 6.9 %collective-permute-done.1 = bf16[48,1280]{1,0:T(8,128)(2,1)S(1)} collective-permute-done((bf16[48,1280]{1,0:T(8,128)(2,1)S(1)}, bf16[48,1280]{1,0:T(8,128)(2,1)S(1)}, u32[]{:S(2)}, u32[]{:S(2)}) %collective-permute-start.1) | collective-permute-done | bytes 122912 | tf_op jit(solution)/shard_map/ppermute | solution.py:62
  34.0 15.4 %collective-permute-done.6 = bf16[48,1536]{1,0:T(8,128)(2,1)} collective-permute-done((bf16[48,1536]{1,0:T(8,128)(2,1)S(1)}, bf16[48,1536]{1,0:T(8,128)(2,1)}, u32[]{:S(2)}, u32[]{:S(2)}) %collective-permute-start.6) | collective-permute-done | bytes 147488 | tf_op jit(solution)/shard_map/ppermute | solution.py:62
  73.7 10.8 %shard_map.376 = (f32[384,768]{1,0:T(8,128)}, bf16[384,768]{1,0:T(8,128)(2,1)}, bf16[384,1152]{1,0:T(8,128)(2,1)}, bf16[384,1152]{1,0:T(8,128)(2,1)}, bf16[384,3...) custom-call(s32[6]{0:T(128)} %pad_add_fusion.1.info, bf16[768,768]{1,0:T(8,128)(2,1)} %tokens.1, ...), custom_call_target="tpu_custom_call" | custom-call | flops 1000 | bytes 1000 | tf_op jit(solution)/shard_map/pallas_call | solution.py:394
  91.3 6.1 %all-to-all-start.1 = ((bf16[16,2,24,384]{3,2,1,0:T(8,128)(2,1)}), bf16[16,2,24,384]{3,2,1,0:T(8,128)(2,1)S(1)}, u32[]{:S(2)}, u32[]{:S(2)}) async-start(bf16[16,2,24,384]{3,2,1,0:T(8,128)(2,1)} %bitcast.136), calls=%async_computation.1 | async-start | bytes 1179648 | tf_op jit(solution)/shard_map/all_to_all | solution.py:218
  102.9 15.2 %collective-permute-done.15.left_ref = bf16[4,48,768]{2,1,0:T(8,128)(2,1)S(1)} collective-permute-done((bf16[4,48,768]{2,1,0:T(8,128)(2,1)S(1)}, bf16[4,48,768]{2,1,0:T(8,128)(2,1)S(1)}, u32[]{:S(2)}, u32[]{:S(2)}) %collective-permute-start.15) | collective-permute-done | bytes 294944 | tf_op jit(solution)/shard_map/ppermute | solution.py:53
  131.8 10.8 %shard_map.379 = (f32[384,768]{1,0:T(8,128)}, bf16[384,768]{1,0:T(8,128)(2,1)}, bf16[384,384]{1,0:T(8,128)(2,1)}, bf16[384,384]{1,0:T(8,128)(2,1)}, bf16[384,768...) custom-call(s32[6]{0:T(128)} %pad_add_fusion.1.info, ...), custom_call_target="tpu_custom_call" | custom-call | flops 1000 | bytes 1000 | tf_op jit(solution)/shard_map/pallas_call | solution.py:394
  143.1 5.8 %collective-permute-done.19 = bf16[2,384,384]{2,1,0:T(8,128)(2,1)S(1)} collective-permute-done((bf16[2,384,384]{2,1,0:T(8,128)(2,1)S(1)}, bf16[2,384,384]{2,1,0:T(8,128)(2,1)S(1)}, u32[]{:S(2)}, u32[]{:S(2)}) %collective-permute-start.19) | collective-permute-done | bytes 589856 | tf_op jit(solution)/shard_map/ppermute | solution.py:49
  152.5 13.8 %shard_map.380 = (f32[384,768]{1,0:T(8,128)}, bf16[384,768]{1,0:T(8,128)(2,1)}, bf16[384,1024]{1,0:T(8,128)(2,1)}, bf16[384,1024]{1,0:T(8,128)(2,1)}, bf16[384,2...) custom-call(s32[6]{0:T(128)} %pad_add_fusion.1.info, ...), custom_call_target="tpu_custom_call" | custom-call | flops 1000 | bytes 1000 | tf_op jit(solution)/shard_map/pallas_call | solution.py:394
  167.0 4.9 %collective-permute-done.20.refs_1_ = bf16[384,768]{1,0:T(8,128)(2,1)S(1)} collective-permute-done((bf16[384,768]{1,0:T(8,128)(2,1)}, bf16[384,768]{1,0:T(8,128)(2,1)S(1)}, u32[]{:S(2)}, u32[]{:S(2)}) %collective-permute-start.20) | collective-permute-done | bytes 589856 | tf_op jit(solution)/shard_map/ppermute | solution.py:49
  173.5 11.3 %shard_map.381 = (bf16[4,48,1536]{2,1,0:T(8,128)(2,1)}, bf16[4,48,1536]{2,1,0:T(8,128)(2,1)}, bf16[3,4,48,3072]{3,2,1,0:T(8,128)(2,1)}) custom-call(s32[6]{0:T(128)} %pad_add_fusion.1.info, bf16[384,768]{1,0:T(8,128)(2,1)} %get-tuple-element.189.refs_0_, bf16[384,768]{1,0:T(8,128)(2,1)} %copy-done.17, ...), custom_call_target="tpu_custom_call" | custom-call | flops 1000 | bytes 1000 | tf_op jit(solution)/shard_map/pallas_call | solution.py:394
  187.6 4.9 %all-to-all-start.2 = ((bf16[16,2,24,384]{3,2,1,0:T(8,128)(2,1)}), bf16[16,2,24,384]{3,2,1,0:T(8,128)(2,1)}, u32[]{:S(2)}, u32[]{:S(2)}) async-start(bf16[16,2,24,384]{3,2,1,0:T(8,128)(2,1)} %maximum_bitcast_fusion.1), calls=%async_computation.2 | async-start | bytes 1179648 | tf_op jit(solution)/shard_map/all_to_all | solution.py:218
  197.1 18.5 %shard_map.382 = (f32[384,768]{1,0:T(8,128)}, bf16[384,768]{1,0:T(8,128)(2,1)}, bf16[384,384]{1,0:T(8,128)(2,1)}, bf16[384,384]{1,0:T(8,128)(2,1)}, bf16[384,768...) custom-call(s32[6]{0:T(128)} %pad_add_fusion.1.info, f32[8,768]{1,0:T(8,128)} %get-tuple-element.167.rows, ...), custom_call_target="tpu_custom_call" | custom-call | flops 1000 | bytes 1000 | tf_op jit(solution)/shard_map/pallas_call | solution.py:394
  221.8 7.0 %all-to-all-start.3 = ((bf16[16,2,24,384]{3,2,1,0:T(8,128)(2,1)}), bf16[16,2,24,384]{3,2,1,0:T(8,128)(2,1)S(1)}, u32[]{:S(2)}, u32[]{:S(2)}) async-start(bf16[16,2,24,384]{3,2,1,0:T(8,128)(2,1)} %bitcast.132), calls=%async_computation.3 | async-start | bytes 1179648 | tf_op jit(solution)/shard_map/all_to_all | solution.py:218
  229.4 7.6 %shard_map.384 = (f32[384,768]{1,0:T(8,128)}, bf16[384,768]{1,0:T(8,128)(2,1)}, bf16[384,384]{1,0:T(8,128)(2,1)}, bf16[384,384]{1,0:T(8,128)(2,1)}, f32[384,768]{1,0:T(8,128)}, /*index=5*/f32[8,768]{1,0:T(8,128)}) custom-call(s32[6]{0:T(128)} %pad_add_fusion.1.info, f32[8,768]{1,0:T(8,128)} %get-tuple-element.167.rows, ...), custom_call_target="tpu_custom_call" | custom-call | flops 1000 | bytes 1000 | tf_op jit(solution)/shard_map/pallas_call | solution.py:394
  240.7 8.9 %shard_map.385 = (bf16[4,48,960]{2,1,0:T(8,128)(2,1)}, bf16[4,48,960]{2,1,0:T(8,128)(2,1)}, bf16[3,4,48,1920]{3,2,1,0:T(8,128)(2,1)}) custom-call(s32[6]{0:T(128)} %pad_add_fusion.1.info, bf16[384,768]{1,0:T(8,128)(2,1)} %get-tuple-element.220.refs_0_, bf16[384,768]{1,0:T(8,128)(2,1)} %collective-permute-done.28.refs_1_, ...), custom_call_target="tpu_custom_call" | custom-call | flops 1000 | bytes 1000 | tf_op jit(solution)/shard_map/pallas_call | solution.py:394
  249.6 6.1 %all-to-all-done.3 = bf16[16,2,24,384]{3,2,1,0:T(8,128)(2,1)S(1)} async-done(((bf16[16,2,24,384]{3,2,1,0:T(8,128)(2,1)}), bf16[16,2,24,384]{3,2,1,0:T(8,128)(2,1)S(1)}, u32[]{:S(2)}, u32[]{:S(2)}) %all-to-all-start.3) | async-done | bytes 589856 | tf_op jit(solution)/shard_map/all_to_all | solution.py:218
  260.2 12.3 %shard_map.386 = (bf16[384,1152]{1,0:T(8,128)(2,1)}, bf16[384,1152]{1,0:T(8,128)(2,1)}, f32[16,512]{1,0:T(8,128)}) custom-call(s32[6]{0:T(128)} %pad_add_fusion.1.info, f32[16,512]{1,0:T(8,128)} %pad.21.window, bf16[384,1152]{1,0:T(8,128)(2,1)} %get-tuple-element.237.qkv_own, bf16[384,1152]{1,0:T(8,128)(2,1)} %get-tuple-element.238.qkv_other, ...), custom_call_target="tpu_custom_call" | custom-call | flops 1000 | bytes 1000 | tf_op jit(solution)/shard_map/pallas_call | solution.py:394
  279.7 6.7 %shard_map.387 = (f32[384,768]{1,0:T(8,128)}, f32[24,768]{1,0:T(8,128)}) custom-call(s32[6]{0:T(128)} %pad_add_fusion.1.info, f32[8,768]{1,0:T(8,128)} %get-tuple-element.167.rows, f32[384,768]{1,0:T(8,128)} %get-tuple-element.166.start, f32[384,768]{1,0:T(8,128)} %get-tuple-element.261.grad_in, bf16[384,1152]{1,0:T(8,128)(2,1)} %get-tuple-element.259.grad_qkv_own.refs_2_, ...), custom_call_target="tpu_custom_call" | custom-call | flops 1000 | bytes 1000 | tf_op jit(solution)/shard_map/pallas_call | solution.py:394
  289.5 5.5 %shard_map.388 = (bf16[4,48,640]{2,1,0:T(8,128)(2,1)}, bf16[4,48,640]{2,1,0:T(8,128)(2,1)}, bf16[3,4,48,1280]{3,2,1,0:T(8,128)(2,1)}) custom-call(s32[6]{0:T(128)} %pad_add_fusion.1.info, bf16[384,768]{1,0:T(8,128)(2,1)} %get-tuple-element.258.refs_0_, bf16[384,768]{1,0:T(8,128)(2,1)} %copy-done.19, ...), custom_call_target="tpu_custom_call" | custom-call | flops 1000 | bytes 1000 | tf_op jit(solution)/shard_map/pallas_call | solution.py:394
  295.0 8.6 %collective-permute-done.40 = bf16[48,3072]{1,0:T(8,128)(2,1)S(1)} collective-permute-done((bf16[48,3072]{1,0:T(8,128)(2,1)S(1)}, bf16[48,3072]{1,0:T(8,128)(2,1)S(1)}, u32[]{:S(2)}, u32[]{:S(2)}) %collective-permute-start.40) | collective-permute-done | bytes 294944 | tf_op jit(solution)/shard_map/ppermute | solution.py:62
  313.8 9.6 %collective-permute-done.37 = bf16[4,48,1920]{2,1,0:T(8,128)(2,1)} collective-permute-done((bf16[4,48,1920]{2,1,0:T(8,128)(2,1)}, bf16[4,48,1920]{2,1,0:T(8,128)(2,1)}, u32[]{:S(2)}, u32[]{:S(2)}) %collective-permute-start.37) | collective-permute-done | bytes 737312 | tf_op jit(solution)/shard_map/ppermute | solution.py:53
  340.5 11.1 %collective-permute-done.56 = bf16[48,1920]{1,0:T(8,128)(2,1)S(1)} collective-permute-done((bf16[48,1920]{1,0:T(8,128)(2,1)S(1)}, bf16[48,1920]{1,0:T(8,128)(2,1)S(1)}, u32[]{:S(2)}, u32[]{:S(2)}) %collective-permute-start.56) | collective-permute-done | bytes 184352 | tf_op jit(solution)/shard_map/ppermute | solution.py:62
  362.3 6.9 %collective-permute-done.53 = bf16[48,1280]{1,0:T(8,128)(2,1)S(1)} collective-permute-done((bf16[48,1280]{1,0:T(8,128)(2,1)S(1)}, bf16[48,1280]{1,0:T(8,128)(2,1)S(1)}, u32[]{:S(2)}, u32[]{:S(2)}) %collective-permute-start.53) | collective-permute-done | bytes 122912 | tf_op jit(solution)/shard_map/ppermute | solution.py:62
  (260 shorter events, 144.6 us)
Async XLA Ops:
  7.2 135.4 %all-gather.2.cloned.1.call-start = ((), (), s32[]{:S(2)}) async-start(), calls=%async_computation.4 | async-start | bytes 5640192 | tf_op jit(solution)/shard_map/all_gather | solution.py:857
  24.9 24.5 %collective-permute-start.3 = (bf16[4,48,1280]{2,1,0:T(8,128)(2,1)S(1)}, bf16[4,48,1280]{2,1,0:T(8,128)(2,1)S(1)}, u32[]{:S(2)}, u32[]{:S(2)}) collective-permute-start(bf16[4,48,1280]{2,1,0:T(8,128)(2,1)S(1)} %pad_maximum_fusion.1.own_ref), channel_id=1, source_target_pairs={{0,2},{2,0},{4,6},{6,4},{8,10},{10,8},{12,14},{14,12},{16,18},{18,... | collective-permute-start | bytes 1474568 | tf_op jit(solution)/shard_map/ppermute | solution.py:53
  26.5 23.6 %collective-permute-start.4 = (bf16[4,48,1280]{2,1,0:T(8,128)(2,1)S(1)}, bf16[4,48,1280]{2,1,0:T(8,128)(2,1)S(1)}, u32[]{:S(2)}, u32[]{:S(2)}) collective-permute-start(bf16[4,48,1280]{2,1,0:T(8,128)(2,1)S(1)} %pad_maximum_fusion.1.own_ref), channel_id=1, source_target_pairs={{0,4},{2,6},{4,0},{6,2},{8,12},{10,14},{12,8},{14,10},{16,20},{18,... | collective-permute-start | bytes 1474568 | tf_op jit(solution)/shard_map/ppermute | solution.py:53
  29.7 19.7 %collective-permute-start.6 = (bf16[48,1536]{1,0:T(8,128)(2,1)S(1)}, bf16[48,1536]{1,0:T(8,128)(2,1)}, u32[]{:S(2)}, u32[]{:S(2)}) collective-permute-start(bf16[48,1536]{1,0:T(8,128)(2,1)S(1)} %pad_maximum_fusion.3), channel_id=1, source_target_pairs={{0,16},{2,18},{4,20},{6,22},{8,24},{10,26},{12,28},{14,30},{16,0},... | collective-permute-start | bytes 442376 | tf_op jit(solution)/shard_map/ppermute | solution.py:62
  61.1 27.1 %all-to-all-start = ((bf16[16,2,24,384]{3,2,1,0:T(8,128)(2,1)}), bf16[16,2,24,384]{3,2,1,0:T(8,128)(2,1)S(1)}, u32[]{:S(2)}, u32[]{:S(2)}) async-start(bf16[16,2,24,384]{3,2,1,0:T(8,128)(2,1)} %maximum_bitcast_fusion), calls=%async_computation | async-start | bytes 1179648 | tf_op jit(solution)/shard_map/all_to_all | solution.py:218
  67.2 20.7 %collective-permute-start.13 = (bf16[4,48,1536]{2,1,0:T(8,128)(2,1)S(1)}, bf16[4,48,1536]{2,1,0:T(8,128)(2,1)}, u32[]{:S(2)}, u32[]{:S(2)}) collective-permute-start(bf16[4,48,1536]{2,1,0:T(8,128)(2,1)S(1)} %pad_maximum_fusion.own_ref), channel_id=1, source_target_pairs={{0,2},{2,0},{4,6},{6,4},{8,10},{10,8},{12,14},{14,12},{16,18},{18,... | collective-permute-start | bytes 1769480 | tf_op jit(solution)/shard_map/ppermute | solution.py:53
  91.3 34.2 %all-to-all-start.1 = ((bf16[16,2,24,384]{3,2,1,0:T(8,128)(2,1)}), bf16[16,2,24,384]{3,2,1,0:T(8,128)(2,1)S(1)}, u32[]{:S(2)}, u32[]{:S(2)}) async-start(bf16[16,2,24,384]{3,2,1,0:T(8,128)(2,1)} %bitcast.136), calls=%async_computation.1 | async-start | bytes 1179648 | tf_op jit(solution)/shard_map/all_to_all | solution.py:218
  98.4 19.7 %collective-permute-start.15 = (bf16[4,48,768]{2,1,0:T(8,128)(2,1)S(1)}, bf16[4,48,768]{2,1,0:T(8,128)(2,1)S(1)}, u32[]{:S(2)}, u32[]{:S(2)}) collective-permute-start(bf16[4,48,768]{2,1,0:T(8,128)(2,1)S(1)} %slice.103), channel_id=1, source_target_pairs={{0,4},{2,6},{4,0},{6,2},{8,12},{10,14},{12,8},{14,10},{16,20},{18,... | collective-permute-start | bytes 884744 | tf_op jit(solution)/shard_map/ppermute | solution.py:53
  101.4 20.3 %collective-permute-start.16 = (bf16[4,48,768]{2,1,0:T(8,128)(2,1)S(1)}, bf16[4,48,768]{2,1,0:T(8,128)(2,1)S(1)}, u32[]{:S(2)}, u32[]{:S(2)}) collective-permute-start(bf16[4,48,768]{2,1,0:T(8,128)(2,1)S(1)} %slice.104), channel_id=1, source_target_pairs={{0,2},{2,0},{4,6},{6,4},{8,10},{10,8},{12,14},{14,12},{16,18},{18,... | collective-permute-start | bytes 884744 | tf_op jit(solution)/shard_map/ppermute | solution.py:53
  187.6 28.0 %all-to-all-start.2 = ((bf16[16,2,24,384]{3,2,1,0:T(8,128)(2,1)}), bf16[16,2,24,384]{3,2,1,0:T(8,128)(2,1)}, u32[]{:S(2)}, u32[]{:S(2)}) async-start(bf16[16,2,24,384]{3,2,1,0:T(8,128)(2,1)} %maximum_bitcast_fusion.1), calls=%async_computation.2 | async-start | bytes 1179648 | tf_op jit(solution)/shard_map/all_to_all | solution.py:218
  192.5 23.2 %collective-permute-start.23 = (bf16[4,48,1536]{2,1,0:T(8,128)(2,1)}, bf16[4,48,1536]{2,1,0:T(8,128)(2,1)}, u32[]{:S(2)}, u32[]{:S(2)}) collective-permute-start(bf16[4,48,1536]{2,1,0:T(8,128)(2,1)} %get-tuple-element.199), channel_id=1, source_target_pairs={{0,2},{2,0},{4,6},{6,4},{8,10},{10,8},{12,14},{14,12},{16,18},{18,... | collective-permute-start | bytes 1769480 | tf_op jit(solution)/shard_map/ppermute | solution.py:53
  194.6 21.1 %collective-permute-start.24 = (bf16[4,48,1536]{2,1,0:T(8,128)(2,1)}, bf16[4,48,1536]{2,1,0:T(8,128)(2,1)}, u32[]{:S(2)}, u32[]{:S(2)}) collective-permute-start(bf16[4,48,1536]{2,1,0:T(8,128)(2,1)} %get-tuple-element.200), channel_id=1, source_target_pairs={{0,4},{2,6},{4,0},{6,2},{8,12},{10,14},{12,8},{14,10},{16,20},{18,... | collective-permute-start | bytes 1769480 | tf_op jit(solution)/shard_map/ppermute | solution.py:53
  196.6 32.2 %collective-permute-start.34 = (bf16[384,384]{1,0:T(8,128)(2,1)}, bf16[384,384]{1,0:T(8,128)(2,1)}, u32[]{:S(2)}, u32[]{:S(2)}) collective-permute-start(bf16[384,384]{1,0:T(8,128)(2,1)} %get-tuple-element.176.attended_other), channel_id=1, source_target_pairs={{0,1},{1,0},{2,3},{3,2},{4,5},{5,4},{6,7},{7,6},{8,9},{9,8},{10,11... | collective-permute-start | bytes 884744 | tf_op jit(solution)/shard_map/ppermute | solution.py:49
  196.6 40.4 %collective-permute-start.28 = (bf16[384,768]{1,0:T(8,128)(2,1)}, bf16[384,768]{1,0:T(8,128)(2,1)}, u32[]{:S(2)}, u32[]{:S(2)}) collective-permute-start(bf16[384,768]{1,0:T(8,128)(2,1)} %get-tuple-element.220.refs_0_), channel_id=1, source_target_pairs={{0,1},{1,0},{2,3},{3,2},{4,5},{5,4},{6,7},{7,6},{8,9},{9,8},{10,11... | collective-permute-start | bytes 1769480 | tf_op jit(solution)/shard_map/ppermute | solution.py:49
  221.0 34.8 %collective-permute-start.26 = (bf16[4,48,3072]{2,1,0:T(8,128)(2,1)}, bf16[4,48,3072]{2,1,0:T(8,128)(2,1)S(1)}, u32[]{:S(2)}, u32[]{:S(2)}) collective-permute-start(bf16[4,48,3072]{2,1,0:T(8,128)(2,1)} %get-tuple-element.218), channel_id=1, source_target_pairs={{0,2},{2,0},{4,6},{6,4},{8,10},{10,8},{12,14},{14,12},{16,18},{18,... | collective-permute-start | bytes 3538952 | tf_op jit(solution)/shard_map/ppermute | solution.py:53
  221.5 34.2 %collective-permute-start.27 = (bf16[4,48,3072]{2,1,0:T(8,128)(2,1)}, bf16[4,48,3072]{2,1,0:T(8,128)(2,1)}, u32[]{:S(2)}, u32[]{:S(2)}) collective-permute-start(bf16[4,48,3072]{2,1,0:T(8,128)(2,1)} %get-tuple-element.219), channel_id=1, source_target_pairs={{0,4},{2,6},{4,0},{6,2},{8,12},{10,14},{12,8},{14,10},{16,20},{18,... | collective-permute-start | bytes 3538952 | tf_op jit(solution)/shard_map/ppermute | solution.py:53
  221.8 33.9 %all-to-all-start.3 = ((bf16[16,2,24,384]{3,2,1,0:T(8,128)(2,1)}), bf16[16,2,24,384]{3,2,1,0:T(8,128)(2,1)S(1)}, u32[]{:S(2)}, u32[]{:S(2)}) async-start(bf16[16,2,24,384]{3,2,1,0:T(8,128)(2,1)} %bitcast.132), calls=%async_computation.3 | async-start | bytes 1179648 | tf_op jit(solution)/shard_map/all_to_all | solution.py:218
  274.6 20.4 %collective-permute-start.39 = (bf16[48,3072]{1,0:T(8,128)(2,1)S(1)}, bf16[48,3072]{1,0:T(8,128)(2,1)S(1)}, u32[]{:S(2)}, u32[]{:S(2)}) collective-permute-start(bf16[48,3072]{1,0:T(8,128)(2,1)S(1)} %get-tuple-element.255), channel_id=1, source_target_pairs={{0,24},{2,26},{4,28},{6,30},{8,0},{10,2},{12,4},{14,6},{16,8},{18,... | collective-permute-start | bytes 884744 | tf_op jit(solution)/shard_map/ppermute | solution.py:62
  277.8 25.8 %collective-permute-start.40 = (bf16[48,3072]{1,0:T(8,128)(2,1)S(1)}, bf16[48,3072]{1,0:T(8,128)(2,1)S(1)}, u32[]{:S(2)}, u32[]{:S(2)}) collective-permute-start(bf16[48,3072]{1,0:T(8,128)(2,1)S(1)} %get-tuple-element.256), channel_id=1, source_target_pairs={{0,16},{2,18},{4,20},{6,22},{8,24},{10,26},{12,28},{14,30},{16,0},... | collective-permute-start | bytes 884744 | tf_op jit(solution)/shard_map/ppermute | solution.py:62
  277.9 25.8 %collective-permute-start.41 = (bf16[48,3072]{1,0:T(8,128)(2,1)S(1)}, bf16[48,3072]{1,0:T(8,128)(2,1)S(1)}, u32[]{:S(2)}, u32[]{:S(2)}) collective-permute-start(bf16[48,3072]{1,0:T(8,128)(2,1)S(1)} %get-tuple-element.257), channel_id=1, source_target_pairs={{0,8},{2,10},{4,12},{6,14},{8,16},{10,18},{12,20},{14,22},{16,24},... | collective-permute-start | bytes 884744 | tf_op jit(solution)/shard_map/ppermute | solution.py:62
  303.7 19.7 %collective-permute-start.37 = (bf16[4,48,1920]{2,1,0:T(8,128)(2,1)}, bf16[4,48,1920]{2,1,0:T(8,128)(2,1)}, u32[]{:S(2)}, u32[]{:S(2)}) collective-permute-start(bf16[4,48,1920]{2,1,0:T(8,128)(2,1)} %get-tuple-element.252), channel_id=1, source_target_pairs={{0,2},{2,0},{4,6},{6,4},{8,10},{10,8},{12,14},{14,12},{16,18},{18,... | collective-permute-start | bytes 2211848 | tf_op jit(solution)/shard_map/ppermute | solution.py:53
  304.6 19.6 %collective-permute-start.38 = (bf16[4,48,1920]{2,1,0:T(8,128)(2,1)}, bf16[4,48,1920]{2,1,0:T(8,128)(2,1)}, u32[]{:S(2)}, u32[]{:S(2)}) collective-permute-start(bf16[4,48,1920]{2,1,0:T(8,128)(2,1)} %get-tuple-element.253), channel_id=1, source_target_pairs={{0,4},{2,6},{4,0},{6,2},{8,12},{10,14},{12,8},{14,10},{16,20},{18,... | collective-permute-start | bytes 2211848 | tf_op jit(solution)/shard_map/ppermute | solution.py:53
  306.0 22.2 %collective-permute-start.45 = (bf16[4,48,640]{2,1,0:T(8,128)(2,1)}, bf16[4,48,640]{2,1,0:T(8,128)(2,1)}, u32[]{:S(2)}, u32[]{:S(2)}) collective-permute-start(bf16[4,48,640]{2,1,0:T(8,128)(2,1)} %get-tuple-element.271), channel_id=1, source_target_pairs={{0,2},{2,0},{4,6},{6,4},{8,10},{10,8},{12,14},{14,12},{16,18},{18,... | collective-permute-start | bytes 737288 | tf_op jit(solution)/shard_map/ppermute | solution.py:53
  307.7 21.0 %collective-permute-start.46 = (bf16[4,48,640]{2,1,0:T(8,128)(2,1)}, bf16[4,48,640]{2,1,0:T(8,128)(2,1)}, u32[]{:S(2)}, u32[]{:S(2)}) collective-permute-start(bf16[4,48,640]{2,1,0:T(8,128)(2,1)} %get-tuple-element.272), channel_id=1, source_target_pairs={{0,4},{2,6},{4,0},{6,2},{8,12},{10,14},{12,8},{14,10},{16,20},{18,... | collective-permute-start | bytes 737288 | tf_op jit(solution)/shard_map/ppermute | solution.py:53
  (78 other events, 641.7 us)
Sparse Core Ops, SparseCore 0:
  24.8 111.8 all-gather.1
